TPU v7x, 1024 devices: a whole 8x8x8 slice. The times are simulated.
1024 devices in a mesh: grid: 64 (over x_hi, z, core), sector: 16 (over x_lo, y).
Axes of the slice: x: 8 (x_hi: 4, x_lo: 2; x = x_hi * 2 + x_lo), y: 8, z: 8, core: 2. Of those that a mesh axis runs over, the one named last changes fastest.
Arguments:
- grid_feat: bfloat16 [131072, 512], P(('grid', 'sector')), may hold values from -6 to 6
- latent: bfloat16 [8192, 1024], P('grid', 'sector'), may hold values from -6 to 6
- query_gain: float32 [512], replicated, may hold values from 0.25 to 1.75
- w_q: bfloat16 [512, 512], replicated, may hold values from -0.25 to 0.25
- w_kv: bfloat16 [1024, 1024], P('sector'), may hold values from -0.1875 to 0.1875
- w_o: bfloat16 [512, 512], replicated, may hold values from -0.25 to 0.25
- head_scale: float32 [8], replicated, may hold values from 0.5 to 80
- block_lists: int32 [1024, 16], P(('grid', 'sector')), may hold values from 0 to 15, as said below
- list_len: int32 [1024], P(('grid', 'sector')), may hold values from 1 to 16, as said below
- dest: int32 [131072], P(('grid', 'sector')), may hold values from 0 to 131071, as said below
Outputs:
- decoded: bfloat16 [131072, 512], P(('grid', 'sector'))
Inputs may be any that keep to these rules, and one draw needn't show every extreme that they name: `block_lists`: each row is an ordering of 0 to 16 - 1 (distinct entries); entries at or past list_len are unused. `list_len`: blocks of the first and last band use all 16 entries; other blocks use at least 1 and at most 4 entries. `dest`: A permutation. The point of row r goes to a device (rows over grid+sector) with the same sector index as r's device, and a device's output slot j comes from the device of band j // 2 in its sector; each source sends 2 rows to each device of its sector.
All inputs are finite; a program needn't handle non-finite values.
Results may differ from a plain program's by a relative error of at most 0.013.
The roundings to bfloat16 on the way count: a program that leaves them out, or rounds other values in their place, can miss the bound.
Values may be sent and summed in bfloat16 or wider, within the bound.
No kernel may reach another device: no remote copies, remote signals or barrier semaphores. Data moves between devices by JAX's collectives and lax.ppermute only.
A program may use at most 32 MiB of HBM per device.

v0:
```python
import math

import jax
import jax.numpy as jnp
from jax import lax
from jax.sharding import PartitionSpec as P

HEADS = 8
BLOCK = 128


def from_partner(block, axis, apart):
    count = lax.axis_size(axis)
    route = []
    for low in range(count):
        high = low | 1 << apart
        if high != low and high < count:
            route += [(low, high), (high, low)]
    return lax.ppermute(block, axis, route)


def layer_norm(features, gains):
    values = features.astype(jnp.float32)
    centred = values - jnp.mean(values, axis=-1, keepdims=True)
    spread = jnp.mean(centred * centred, axis=-1, keepdims=True)
    return (centred * lax.rsqrt(spread + 1e-05) * gains).astype(jnp.bfloat16)


def gather_group(panels, band_index, bit_count):
    sequence = list(range(bit_count))
    for bit_number in sequence:
        partner = from_partner(panels, "grid", bit_number)
        is_upper = band_index // (1 << bit_number) % 2 == 1
        lower_half = jnp.where(is_upper, partner, panels)
        upper_half = jnp.where(is_upper, panels, partner)
        panels = jnp.concatenate([lower_half, upper_half], axis=0)
    return panels


def shards(grid_feat, latent, query_gain, w_q, w_kv, w_o, head_scale, block_lists, list_len, dest):
    sector_count = lax.axis_size("sector")
    band_count = lax.axis_size("grid")
    group_size = band_count // 4
    bit_count = group_size.bit_length() - 1
    band_index = lax.axis_index("grid")
    model_width = grid_feat.shape[1]
    head_dim = model_width // HEADS
    partial_sum = jnp.dot(latent, w_kv, preferred_element_type=jnp.float32)
    panels = lax.psum(partial_sum, "sector").astype(jnp.bfloat16)
    stacked = gather_group(panels[None], band_index, bit_count)
    key_value = stacked.reshape(group_size, BLOCK, 2, HEADS, head_dim)
    normed = layer_norm(grid_feat, query_gain)
    queries = jnp.dot(normed, w_q, preferred_element_type=jnp.float32).astype(jnp.bfloat16)
    query_blocks = queries.reshape(-1, BLOCK, HEADS, head_dim)
    score_scale = head_scale / math.sqrt(head_dim)
    entry_slots = jnp.arange(group_size, dtype=jnp.int32)

    def attend(operands):
        query_block, entries, length = operands
        chosen = key_value[entries]
        keys = chosen[:, :, 0].reshape(group_size * BLOCK, HEADS, head_dim)
        values = chosen[:, :, 1].reshape(group_size * BLOCK, HEADS, head_dim)
        scores = jnp.einsum("qhd,khd->hqk", query_block, keys, preferred_element_type=jnp.float32)
        scores = scores * score_scale[:, None, None]
        valid = jnp.repeat(entry_slots < length, BLOCK)
        scores = jnp.where(valid[None, None, :], scores, -jnp.inf)
        row_max = jnp.max(scores, axis=-1, keepdims=True)
        weights = jnp.exp(scores - row_max)
        denominator = jnp.sum(weights, axis=-1)
        probs = weights.astype(jnp.bfloat16)
        weighted = jnp.einsum("hqk,khd->hqd", probs, values, preferred_element_type=jnp.float32)
        attended = weighted / denominator[:, :, None]
        return attended.transpose(1, 0, 2).reshape(BLOCK, model_width).astype(jnp.bfloat16)

    attended = lax.map(attend, (query_blocks, block_lists, list_len)).reshape(-1, model_width)
    updated = (
        grid_feat.astype(jnp.float32) + jnp.dot(attended, w_o, preferred_element_type=jnp.float32)
    ).astype(jnp.bfloat16)
    local_rows = grid_feat.shape[0]
    per_band = local_rows // band_count
    target_band = dest // local_rows // sector_count
    slot_index = dest % local_rows - band_index * per_band
    position = target_band * per_band + slot_index
    outgoing = jnp.zeros_like(updated).at[position].set(updated)
    return lax.all_to_all(outgoing, "grid", split_axis=0, concat_axis=0, tiled=True)


def solution(mesh):
    return jax.shard_map(
        shards,
        mesh=mesh,
        in_specs=(
            P(("grid", "sector"), None),
            P("grid", "sector"),
            P(),
            P(),
            P("sector", None),
            P(),
            P(),
            P(("grid", "sector"), None),
            P(("grid", "sector")),
            P(("grid", "sector")),
        ),
        out_specs=P(("grid", "sector"), None),
        check_vma=False,
    )
```

profile of v0, /device:TPU:1, one launch (start us, length us, event | category | flops | bytes accessed | tf_op | source)
XLA Modules:
  0.0 316.0 jit_solution(15818076962159756189)
XLA Ops:
  0.0 0.0 copy-start
  0.0 1.2 fusion.32
  1.2 58.0 %all-reduce.1 = bf16[128,1024]{1,0:T(8,128)(2,1)S(1)} all-reduce(f32[128,1024]{1,0:T(8,128)S(1)} %fusion.32), channel_id=1, replica_groups=mesh['grid'=64,'sector'=16] {'sector'}, use_global_device_ids=true, to_apply=%region_2.3 | all-reduce | flops 131072 | bytes 786432 | tf_op jit(solution)/shard_map/psum | solution.py:49
  59.2 23.8 %collective-permute-start = (bf16[1,128,1024]{2,1,0:T(8,128)(2,1)S(1)}, bf16[1,128,1024]{2,1,0:T(8,128)(2,1)S(1)}, u32[]{:S(2)}, u32[]{:S(2)}) collective-permute-start(bf16[1,128,1024]{2,1,0:T(8,128)(2,1)S(1)} %bitcast.40), channel_id=1, source_target_pairs={{0,16},{16,0},{32,48},{48,32},{64,80},{80,64},{96,112},{112,96},{1... | collective-permute-start | bytes 786440 | tf_op jit(solution)/shard_map/ppermute | solution.py:19
  83.0 1.1 collective-permute-done
  84.2 0.1 pad_maximum_fusion.3
  84.2 1.9 collective-permute-start.1
  86.2 13.0 %collective-permute-done.1 = bf16[2,128,1024]{2,1,0:T(8,128)(2,1)S(1)} collective-permute-done((bf16[2,128,1024]{2,1,0:T(8,128)(2,1)S(1)}, bf16[2,128,1024]{2,1,0:T(8,128)(2,1)S(1)}, u32[]{:S(2)}, u32[]{:S(2)}) %collective-permute-start.1) | collective-permute-done | bytes 524320 | tf_op jit(solution)/shard_map/ppermute | solution.py:19
  99.2 0.1 broadcast_select_fusion.5
  99.3 0.0 copy-start.1
  99.3 0.8 copy-done.1
  100.1 0.1 pad_maximum_fusion.2
  100.2 1.9 collective-permute-start.2
  102.2 0.0 copy-start.3
  102.2 0.0 copy-start.5
  102.2 0.0 copy-start.6
  102.2 0.0 copy-start.7
  102.2 0.0 copy-start.8
  102.2 48.4 %collective-permute-done.2 = bf16[4,128,1024]{2,1,0:T(8,128)(2,1)} collective-permute-done((bf16[4,128,1024]{2,1,0:T(8,128)(2,1)S(1)}, bf16[4,128,1024]{2,1,0:T(8,128)(2,1)}, u32[]{:S(2)}, u32[]{:S(2)}) %collective-permute-start.2) | collective-permute-done | bytes 1048608 | tf_op jit(solution)/shard_map/ppermute | solution.py:19
  150.6 1.5 broadcast_select_fusion.3
  152.1 1.5 pad_maximum_fusion.1
  153.7 8.3 %collective-permute-start.3 = (bf16[8,128,1024]{2,1,0:T(8,128)(2,1)}, bf16[8,128,1024]{2,1,0:T(8,128)(2,1)}, u32[]{:S(2)}, u32[]{:S(2)}) collective-permute-start(bf16[8,128,1024]{2,1,0:T(8,128)(2,1)} %pad_maximum_fusion.1), channel_id=1, source_target_pairs={{0,128},{128,0},{16,144},{144,16},{32,160},{160,32},{48,176},{176,... | collective-permute-start | bytes 6291464 | tf_op jit(solution)/shard_map/ppermute | solution.py:19
  162.6 0.0 copy-done.3
  162.6 0.1 convert_reduce_fusion
  162.7 0.2 fusion.18
  162.9 0.0 copy-done
  163.0 0.0 copy-done.5
  163.0 0.3 convolution_convert_fusion
  163.2 0.1 copy.14
  163.4 0.0 copy-done.6
  163.4 0.0 copy-done.7
  163.4 0.0 copy-done.8
  163.5 0.1 broadcast_bitcast_fusion
  163.5 88.7 %collective-permute-done.3 = bf16[8,128,1024]{2,1,0:T(8,128)(2,1)} collective-permute-done((bf16[8,128,1024]{2,1,0:T(8,128)(2,1)}, bf16[8,128,1024]{2,1,0:T(8,128)(2,1)}, u32[]{:S(2)}, u32[]{:S(2)}) %collective-permute-start.3) | collective-permute-done | bytes 2097184 | tf_op jit(solution)/shard_map/ppermute | solution.py:19
  252.2 1.9 broadcast_select_fusion.1
  254.1 2.3 pad_maximum_fusion
  256.4 6.4 %copy.15 = bf16[16,128,1024]{1,2,0:T(8,128)(2,1)} copy(bf16[16,128,1024]{2,1,0:T(8,128)(2,1)} %pad_maximum_fusion) | data formatting | bytes 8388608 | tf_op jit(solution)/shard_map/concatenate | solution.py:36
  262.8 5.2 %gather_fusion = bf16[16,128,2,8,64]{1,4,3,2,0:T(8,128)(2,1)} fusion(bf16[16,128,2,8,64]{1,4,3,2,0:T(8,128)(2,1)} %bitcast.39, s32[1024]{0:T(1024)S(1)} %pad_clamp_fusion), kind=kCustom, calls=%fused_computation | custom fusion | bytes 8388672 | tf_op jit(solution)/shard_map/while/body/eval_jaxpr/gather | solution.py:60
  268.1 4.7 %fusion.31 = (bf16[16,128,1,8,64]{1,4,3,2,0:T(8,128)(2,1)S(1)}, bf16[16,128,1,8,64]{1,4,3,2,0:T(8,128)(2,1)}) fusion(bf16[16,128,2,8,64]{1,4,3,2,0:T(8,128)(2,1)} %gather_fusion), kind=kLoop, calls=%fused_computation.61 | loop fusion | bytes 8388608 | tf_op jit(solution)/shard_map/while/body/eval_jaxpr/slice | solution.py:61
  272.8 1.4 copy.16
  274.1 2.3 squeeze.26
  276.4 3.0 copy.17
  279.4 2.3 squeeze.27
  281.7 3.0 fusion
  284.7 0.0 copy-start.2
  284.7 1.9 fusion.1
  286.6 0.0 copy-done.2
  286.6 0.0 copy-start.4
  286.7 2.2 fusion.13
  288.9 0.0 copy-done.4
  288.9 0.3 fusion.9
  289.2 1.1 scatter_custom_fusion
  290.3 0.1 all_to_all.8
  290.3 25.0 %all_to_all.12 = bf16[64,2,512]{2,1,0:T(2,128)(2,1)S(1)} all-to-all(bf16[64,2,512]{2,1,0:T(2,128)(2,1)S(1)} %all_to_all.8), channel_id=1, replica_groups=mesh['grid'=64,'sector'=16] {'grid'}, dimensions={0} | all-to-all | bytes 262144 | tf_op jit(solution)/shard_map/all_to_all | solution.py:85
  315.3 0.7 all_to_all.10
  (8 shorter events, 0.1 us)
Async XLA Ops:
  0.0 162.9 %copy-start = (bf16[512,512]{1,0:T(8,128)(2,1)S(1)}, bf16[512,512]{1,0:T(8,128)(2,1)}, u32[]{:S(2)}) copy-start(bf16[512,512]{1,0:T(8,128)(2,1)} %param.13) | copy-start | bytes 1572868
  59.2 24.9 %collective-permute-start = (bf16[1,128,1024]{2,1,0:T(8,128)(2,1)S(1)}, bf16[1,128,1024]{2,1,0:T(8,128)(2,1)S(1)}, u32[]{:S(2)}, u32[]{:S(2)}) collective-permute-start(bf16[1,128,1024]{2,1,0:T(8,128)(2,1)S(1)} %bitcast.40), channel_id=1, source_target_pairs={{0,16},{16,0},{32,48},{48,32},{64,80},{80,64},{96,112},{112,96},{1... | collective-permute-start | bytes 786440 | tf_op jit(solution)/shard_map/ppermute | solution.py:19
  84.2 15.0 %collective-permute-start.1 = (bf16[2,128,1024]{2,1,0:T(8,128)(2,1)S(1)}, bf16[2,128,1024]{2,1,0:T(8,128)(2,1)S(1)}, u32[]{:S(2)}, u32[]{:S(2)}) collective-permute-start(bf16[2,128,1024]{2,1,0:T(8,128)(2,1)S(1)} %pad_maximum_fusion.3), channel_id=1, source_target_pairs={{0,32},{32,0},{16,48},{48,16},{64,96},{96,64},{80,112},{112,80},{1... | collective-permute-start | bytes 1572872 | tf_op jit(solution)/shard_map/ppermute | solution.py:19
  99.3 0.8 copy-start.1
  100.2 50.4 %collective-permute-start.2 = (bf16[4,128,1024]{2,1,0:T(8,128)(2,1)S(1)}, bf16[4,128,1024]{2,1,0:T(8,128)(2,1)}, u32[]{:S(2)}, u32[]{:S(2)}) collective-permute-start(bf16[4,128,1024]{2,1,0:T(8,128)(2,1)S(1)} %pad_maximum_fusion.2), channel_id=1, source_target_pairs={{0,64},{64,0},{16,80},{80,16},{32,96},{96,32},{48,112},{112,48},{1... | collective-permute-start | bytes 3145736 | tf_op jit(solution)/shard_map/ppermute | solution.py:19
  102.2 60.4 %copy-start.3 = (bf16[128,512]{1,0:T(8,128)(2,1)S(1)}, bf16[128,512]{1,0:T(8,128)(2,1)}, u32[]{:S(2)}) copy-start(bf16[128,512]{1,0:T(8,128)(2,1)} %param.10) | copy-start | bytes 393220
  102.2 60.8 %copy-start.5 = (f32[512]{0:T(512)S(1)}, f32[512]{0:T(512)}, u32[]{:S(2)}) copy-start(f32[512]{0:T(512)} %param.12) | copy-start | bytes 6148
  102.2 61.2 %copy-start.6 = (s32[1,16]{1,0:T(1,128)S(1)}, s32[1,16]{1,0:T(1,128)}, u32[]{:S(2)}) copy-start(s32[1,16]{1,0:T(1,128)} %param.17) | copy-start | bytes 196
  102.2 61.2 %copy-start.7 = (f32[8]{0:T(128)S(1)}, f32[8]{0:T(128)}, u32[]{:S(2)}) copy-start(f32[8]{0:T(128)} %param.16) | copy-start | bytes 100
  102.2 61.2 %copy-start.8 = (s32[128]{0:T(128)S(1)}, s32[128]{0:T(128)}, u32[]{:S(2)}) copy-start(s32[128]{0:T(128)} %param.19) | copy-start | bytes 1540
  153.7 98.6 %collective-permute-start.3 = (bf16[8,128,1024]{2,1,0:T(8,128)(2,1)}, bf16[8,128,1024]{2,1,0:T(8,128)(2,1)}, u32[]{:S(2)}, u32[]{:S(2)}) collective-permute-start(bf16[8,128,1024]{2,1,0:T(8,128)(2,1)} %pad_maximum_fusion.1), channel_id=1, source_target_pairs={{0,128},{128,0},{16,144},{144,16},{32,160},{160,32},{48,176},{176,... | collective-permute-start | bytes 6291464 | tf_op jit(solution)/shard_map/ppermute | solution.py:19
  284.7 1.9 copy-start.2
  286.6 2.3 copy-start.4
where the time goes:
time: 317 us; the launch traced here: 316 us
  waiting for transfers between devices  151 us (48%)
  blocking collectives  83 us (26%)
  starting transfers between devices  35.9 us (11%)
  local copies, waits for them, and re-layouts  28.1 us (9%)
  other arithmetic  9.74 us (3%)
  matrix products  6.97 us (2%)
    ppermute x4, waiting for transfers between devices, from_partner(): return lax.ppermute(block, axis, route)  151 us
    psum x1, blocking collectives, shards(): panels = lax.psum(partial_sum, 'sector').astype(jnp.bfloat16)  58 us
    ppermute x4, starting transfers between devices, from_partner(): return lax.ppermute(block, axis, route)  35.9 us
    all_to_all x1, blocking collectives, shards(): lax.all_to_all(outgoing, 'grid', split_axis=0, concat_axis=0, tiled=True)  25 us
    concatenate x1, local copies, waits for them, and re-layouts, gather_group(): panels = jnp.concatenate([lower_half, upper_half], axis=0)  6.39 us
  transfers between devices with their start and end apart: 4, of which 4 were waited for; matrix products, arithmetic and copies ran while one was open for 0% of the time, Pallas kernels for 0%

commit v1 on v0

v1 whole, which is shorter than its diff:
```python
import math

import jax
import jax.numpy as jnp
from jax import lax
from jax.experimental import pallas as pl
from jax.experimental.pallas import tpu as pltpu
from jax.sharding import Mesh, PartitionSpec as P

HEADS = 8
BLOCK = 128
HEAD_DIM = 64
HALF = 64
LISTED = 4
ROWS = 136
SECTORS = 16
GROUP = 16

VMEM = pl.BlockSpec(memory_space=pltpu.VMEM)
SMEM = pl.BlockSpec(memory_space=pltpu.SMEM)


def low_lanes(shape):
    return lax.broadcasted_iota(jnp.int32, shape, len(shape) - 1) < HALF


def swap_halves(x):
    return jnp.concatenate([x[:, HALF:], x[:, :HALF]], axis=1)


def pack_kernel(feat_ref, gain_ref, wq_ref, lat_ref, wkv_ref, list_ref, len_ref, out_ref):
    values = feat_ref[...].astype(jnp.float32)
    centred = values - jnp.mean(values, axis=-1, keepdims=True)
    spread = jnp.mean(centred * centred, axis=-1, keepdims=True)
    normed = (centred * lax.rsqrt(spread + 1e-05) * gain_ref[...]).astype(jnp.bfloat16)
    queries = jnp.dot(normed, wq_ref[...], preferred_element_type=jnp.float32).astype(jnp.bfloat16)
    lane = lax.broadcasted_iota(jnp.int32, (8, 128), 1)
    entries = jnp.where(lane == GROUP, len_ref[0], 0)
    for j in range(GROUP):
        entries = jnp.where(lane == j, list_ref[0, j], entries)
    entries = entries.astype(jnp.float32).astype(jnp.bfloat16)
    low = low_lanes((HALF, 128))
    lat = lat_ref[...]
    swapped = swap_halves(lat)
    for head in range(HEADS):
        tile = slice(head // 2 * 128, head // 2 * 128 + 128)
        key_tile = wkv_ref[:, tile]
        value_tile = wkv_ref[:, slice(tile.start + 512, tile.stop + 512)]
        if head % 2:
            piece = jnp.where(low, swap_halves(key_tile), value_tile)
        else:
            piece = jnp.where(low, key_tile, swap_halves(value_tile))
        for half in range(2):
            query = queries[half * HALF:half * HALF + HALF, tile]
            if head % 2:
                query = swap_halves(query)
            peer = half * HEADS + head
            out_ref[peer, 0:HALF] = jnp.where(low, query, lat if half else swapped)
            out_ref[peer, HALF:2 * HALF] = piece
            out_ref[peer, 2 * HALF:ROWS] = entries


def project_kernel(got_ref, out_ref, table_ref):
    latent = got_ref[:, 0:HALF, :].reshape(SECTORS * HALF, 128)
    weights = got_ref[:, HALF:2 * HALF, :].reshape(SECTORS * HALF, 128)
    product = lax.dot_general(latent, weights, (((0,), (0,)), ((), ())), preferred_element_type=jnp.float32)
    panel = product[HALF:].astype(jnp.bfloat16)
    for peer in range(out_ref.shape[0]):
        out_ref[peer] = panel
    for source in range(SECTORS):
        row = got_ref[source, 2 * HALF:ROWS, :].astype(jnp.float32).astype(jnp.int32)
        table_ref[source:source + 1] = row[0:1]


def attend_kernel(table_ref, head_ref, scale_ref, got_ref, panel_ref, out_ref):
    scale = scale_ref[head_ref[0]] * (1.0 / math.sqrt(HEAD_DIM))
    contract_last = (((1,), (1,)), ((), ()))

    def finish(source, weighted, denominator):
        attended = (weighted / denominator).astype(jnp.bfloat16)
        upper, lower = attended[0:32], attended[32:64]
        out_ref[source] = jnp.where(low_lanes((32, 128)), swap_halves(upper), lower)

    def query_of(source):
        tile = got_ref[source, 0:HALF]
        return jnp.where(low_lanes((HALF, 128)), tile, jnp.zeros_like(tile))

    dense = table_ref[0, GROUP] > LISTED

    @pl.when(dense)
    def _():
        per_step = 4

        @pl.loop(0, SECTORS // per_step)
        def _(step):
            keys = panel_ref[...].reshape(GROUP * BLOCK, 128)
            query = jnp.concatenate([query_of(step * per_step + k) for k in range(per_step)], axis=0)
            scores = lax.dot_general(query, keys, contract_last, preferred_element_type=jnp.float32) * scale
            weights = jnp.exp(scores - jnp.max(scores, axis=-1, keepdims=True))
            denominator = jnp.sum(weights, axis=-1, keepdims=True)
            weighted = jnp.dot(weights.astype(jnp.bfloat16), keys, preferred_element_type=jnp.float32)
            for k in range(per_step):
                rows = slice(k * HALF, k * HALF + HALF)
                finish(step * per_step + k, weighted[rows], denominator[rows])

    @pl.when(jnp.logical_not(dense))
    def _():
        def one(source):
            query = query_of(source)
            blocks, scores = [], []
            for j in range(LISTED):
                entry = table_ref[source, j]
                core, column = entry % 2, entry // 2
                block = jnp.concatenate([panel_ref[core, column], panel_ref[core, HEADS + column]], axis=0)
                score = lax.dot_general(query, block, contract_last, preferred_element_type=jnp.float32) * scale
                if j:
                    score = jnp.where(j < table_ref[source, GROUP], score, -jnp.inf)
                blocks.append(block)
                scores.append(score)
            top = scores[0]
            for score in scores[1:]:
                top = jnp.maximum(top, score)
            top = jnp.max(top, axis=-1, keepdims=True)
            weights = [jnp.exp(score - top) for score in scores]
            denominator = jnp.sum(sum(weights[1:], weights[0]), axis=-1, keepdims=True)
            weighted = sum(
                jnp.dot(weight.astype(jnp.bfloat16), block, preferred_element_type=jnp.float32)
                for weight, block in zip(weights, blocks)
            )
            finish(source, weighted, denominator)

        @pl.loop(0, SECTORS // 4)
        def _(step):
            for k in range(4):
                one(step * 4 + k)


def finish_kernel(got_ref, wo_ref, feat_ref, position_ref, out_ref):
    low = low_lanes((32, 128))
    rows = []
    for half in range(2):
        upper, lower = [], []
        for pair in range(HEADS // 2):
            even = got_ref[half * HEADS + 2 * pair]
            odd = got_ref[half * HEADS + 2 * pair + 1]
            upper.append(jnp.where(low, even, swap_halves(odd)))
            lower.append(jnp.where(low, swap_halves(even), odd))
        rows += [jnp.concatenate(upper, axis=1), jnp.concatenate(lower, axis=1)]
    attended = jnp.concatenate(rows, axis=0)
    product = jnp.dot(attended, wo_ref[...], preferred_element_type=jnp.float32)
    updated = (feat_ref[...].astype(jnp.float32) + product).astype(jnp.bfloat16)
    slot = lax.broadcasted_iota(jnp.int32, (BLOCK, BLOCK), 0)
    chosen = (slot == position_ref[...]).astype(jnp.float32).astype(jnp.bfloat16)
    out_ref[...] = jnp.dot(chosen, updated, preferred_element_type=jnp.float32).astype(jnp.bfloat16)


def shards(grid_feat, latent, query_gain, w_q, w_kv, w_o, head_scale, block_lists, list_len, dest):
    band_axes, sector_axes = ("xh", "z", "c"), ("xl", "y")
    band_count = lax.axis_size(band_axes)
    band_index = lax.axis_index(band_axes)
    local_rows, width = grid_feat.shape
    bf16 = jnp.bfloat16

    packed = pl.pallas_call(
        pack_kernel,
        out_shape=jax.ShapeDtypeStruct((SECTORS, ROWS, 128), bf16),
        in_specs=[VMEM, VMEM, VMEM, VMEM, VMEM, SMEM, SMEM],
        out_specs=VMEM,
        name="pack",
    )(grid_feat, query_gain.reshape(1, -1), w_q, latent.T, w_kv, block_lists, list_len)
    got = lax.all_to_all(packed, sector_axes, 0, 0, tiled=True)

    panel, table = pl.pallas_call(
        project_kernel,
        out_shape=(
            jax.ShapeDtypeStruct((GROUP, HALF, 128), bf16),
            jax.ShapeDtypeStruct((SECTORS, 128), jnp.int32),
        ),
        in_specs=[VMEM],
        out_specs=(VMEM, VMEM),
        name="project",
    )(got)
    panels = lax.all_to_all(panel, ("xl", "z"), 0, 0, tiled=True)
    panels = lax.all_gather(panels, "c", axis=0)

    attended = pl.pallas_call(
        attend_kernel,
        out_shape=jax.ShapeDtypeStruct((SECTORS, 32, 128), bf16),
        in_specs=[SMEM, SMEM, SMEM, VMEM, VMEM],
        out_specs=VMEM,
        name="attend",
    )(table, lax.axis_index("y").reshape(1), head_scale, got, panels)
    attended = lax.all_to_all(attended, sector_axes, 0, 0, tiled=True)

    per_band = local_rows // band_count
    position = dest // local_rows // SECTORS * per_band + dest % local_rows - band_index * per_band
    outgoing = pl.pallas_call(
        finish_kernel,
        out_shape=jax.ShapeDtypeStruct((local_rows, width), bf16),
        in_specs=[VMEM, VMEM, VMEM, VMEM],
        out_specs=VMEM,
        name="finish",
    )(attended, w_o, grid_feat, position.reshape(1, -1))
    return lax.all_to_all(outgoing, band_axes, 0, 0, tiled=True)


def solution(mesh):
    fine = Mesh(mesh.devices.reshape(4, 8, 2, 2, 8), ("xh", "z", "c", "xl", "y"))
    band, sector = ("xh", "z", "c"), ("xl", "y")
    return jax.shard_map(
        shards,
        mesh=fine,
        in_specs=(
            P(band + sector, None),
            P(band, sector),
            P(),
            P(),
            P(sector, None),
            P(),
            P(),
            P(band + sector, None),
            P(band + sector),
            P(band + sector),
        ),
        out_specs=P(band + sector, None),
        check_vma=False,
    )
```

time: 317 us -> 109 us (0.34)
  waiting for transfers between devices: 151 us -> 14.6 us
  blocking collectives: 83 us -> 48.5 us
  local copies, waits for them, and re-layouts: 28.1 us -> 2.98 us
  Pallas kernels: 0 us -> 14.3 us
  other arithmetic: 9.74 us -> 0.56 us
  starting transfers between devices: 35.9 us -> 26.9 us
  matrix products: 6.97 us -> 0 us
    ppermute x4 -> x0, waiting for transfers between devices: 151 us -> none  [from_partner(): return lax.ppermute(block, axis, route)]
    psum x1 -> x0, blocking collectives: 58 us -> none  [shards(): panels = lax.psum(partial_sum, 'sector').astype(jnp.bfloat16)]
    ppermute x4 -> x0, starting transfers between devices: 35.9 us -> none  [from_partner(): return lax.ppermute(block, axis, route)]
    all_to_all x0 -> x2, starting transfers between devices: none -> 26.9 us  [the longest x1 23.4 us: shards(): panels = lax.all_to_all(panel, ('xl', 'z'), 0, 0, tiled=True)]
    all_to_all x1 -> x2, blocking collectives: 25 us -> 43.7 us  [the longest x1 22.2 us: shards(): return lax.all_to_all(outgoing, band_axes, 0, 0, tiled=True)]
    all_to_all x0 -> x2, waiting for transfers between devices: none -> 14.6 us  [the longest x1 8.15 us: shards(): panels = lax.all_to_all(panel, ('xl', 'z'), 0, 0, tiled=True)]
    pallas_call x0 -> x4, Pallas kernels: none -> 14.3 us  [the longest x1 7.65 us: shards(): pl.pallas_call(attend_kernel, out_shape=jax.ShapeDtypeStruct((SECTORS, 32...]
    slice x3 -> x0, local copies, waits for them, and re-layouts: 9.02 us -> none  [the longest x2 6.07 us: attend(): keys = chosen[:, :, 0].reshape(group_size * BLOCK, HEADS, head_dim)]
  transfers between devices with their start and end apart: 4 -> 2, of which waited for: 4 -> 2; matrix products, arithmetic and copies ran while one was open for 0% -> 1% of each run, Pallas kernels for 0% -> 0%
where the time goes in v1:
time: 109 us
  blocking collectives  48.5 us (44%)
  starting transfers between devices  26.9 us (25%)
  waiting for transfers between devices  14.6 us (13%)
  Pallas kernels  14.3 us (13%)
  local copies, waits for them, and re-layouts  2.98 us (3%)
    all_to_all x1, starting transfers between devices, shards(): panels = lax.all_to_all(panel, ('xl', 'z'), 0, 0, tiled=True)  23.4 us
    all_to_all x1, blocking collectives, shards(): return lax.all_to_all(outgoing, band_axes, 0, 0, tiled=True)  22.2 us
    all_to_all x1, blocking collectives, shards(): got = lax.all_to_all(packed, sector_axes, 0, 0, tiled=True)  21.6 us
    all_to_all x1, waiting for transfers between devices, shards(): panels = lax.all_to_all(panel, ('xl', 'z'), 0, 0, tiled=True)  8.15 us
    pallas_call x1, Pallas kernels, shards(): pl.pallas_call(attend_kernel, out_shape=jax.ShapeDtypeStruct((SECTORS, 32...  7.65 us
    all_to_all x1, waiting for transfers between devices, shards(): attended = lax.all_to_all(attended, sector_axes, 0, 0, tiled=True)  6.46 us
    all_gather x1, blocking collectives, shards(): panels = lax.all_gather(panels, 'c', axis=0)  4.73 us
    all_to_all x1, starting transfers between devices, shards(): attended = lax.all_to_all(attended, sector_axes, 0, 0, tiled=True)  3.51 us
  transfers between devices with their start and end apart: 2, of which 2 were waited for; matrix products, arithmetic and copies ran while one was open for 1% of the time, Pallas kernels for 0%

profile of v1, /device:TPU:1, one launch (start us, length us, event | category | flops | bytes accessed | tf_op | source)
XLA Modules:
  0.0 108.6 jit_solution(13890296888853004331)
XLA Ops:
  0.7 2.4 %pack.1 = bf16[16,136,128]{2,1,0:T(8,128)(2,1)} custom-call(bf16[128,512]{1,0:T(8,128)(2,1)} %feat_ref.3, f32[1,512]{1,0:T(1,128)} %bitcast.8, bf16[512,512]{1,0:T(8,128)(2,1)} %wq_ref.1, bf16[64,128]{1,0:T(8,128)(2,1)} %bitcast.7, bf16[64,1024]{1,0:T(8,128)(2,1)} %wkv_ref.1, s32[1,16]{1,0:T(1,128)} %list_ref.1, s32[1]{0:T(128)S(6)} %copy.11.len_ref), custom_call_target="tpu_custom_call" | custom-call | tf_op jit(solution)/shard_map/pack/pallas_call | solution.py:164
  3.1 21.6 %all_to_all.27.got_ref = bf16[16,136,128]{2,1,0:T(8,128)(2,1)} all-to-all(bf16[16,136,128]{2,1,0:T(8,128)(2,1)} %pack.1), channel_id=1, replica_groups=mesh['xh'=4,'z'=8,'c'=2,'xl'=2,'y'=8] {'xl','y'}, dimensions={0} | all-to-all | bytes 1114112 | tf_op jit(solution)/shard_map/all_to_all | solution.py:171
  24.6 2.0 %project.1 = (bf16[16,64,128]{2,1,0:T(8,128)(2,1)}, s32[16,128]{1,0:T(8,128)}) custom-call(bf16[16,136,128]{2,1,0:T(8,128)(2,1)} %all_to_all.27.got_ref), custom_call_target="tpu_custom_call" | custom-call | tf_op jit(solution)/shard_map/project/pallas_call | solution.py:173
  26.7 23.4 %all-to-all-start.1 = ((bf16[16,64,128]{2,1,0:T(8,128)(2,1)}), bf16[16,64,128]{2,1,0:T(8,128)(2,1)S(1)}, u32[]{:S(2)}, u32[]{:S(2)}) async-start(bf16[16,64,128]{2,1,0:T(8,128)(2,1)} %get-tuple-element.8), calls=%async_computation.1 | async-start | bytes 524288 | tf_op jit(solution)/shard_map/all_to_all | solution.py:183
  50.1 8.2 %all-to-all-done.1 = bf16[16,64,128]{2,1,0:T(8,128)(2,1)S(1)} async-done(((bf16[16,64,128]{2,1,0:T(8,128)(2,1)}), bf16[16,64,128]{2,1,0:T(8,128)(2,1)S(1)}, u32[]{:S(2)}, u32[]{:S(2)}) %all-to-all-start.1) | async-done | bytes 262176 | tf_op jit(solution)/shard_map/all_to_all | solution.py:183
  58.3 4.7 %all-gather = bf16[32,64,128]{2,1,0:T(8,128)(2,1)} all-gather(bf16[16,64,128]{2,1,0:T(8,128)(2,1)S(1)} %all-to-all-done.1), channel_id=2, replica_groups=mesh['xh'=4,'z'=8,'c'=2,'xl'=2,'y'=8] {'c'}, dimensions={0}, use_global_device_ids=true | all-gather | bytes 786432 | tf_op jit(solution)/shard_map/all_gather | solution.py:184
  63.0 7.6 %attend.1 = bf16[16,32,128]{2,1,0:T(8,128)(2,1)} custom-call(s32[16,128]{1,0:T(8,128)} %get-tuple-element.7.table_ref, s32[1]{0:T(128)} %bitcast.2.head_ref, f32[8]{0:T(128)} %scale_ref.1, bf16[16,136,128]{2,1,0:T(8,128)(2,1)} %all_to_all.27.got_ref, bf16[2,16,64,128]{3,2,1,0:T(8,128)(2,1)} %bitcast.6), custom_call_target="tpu_custom_call" | custom-call | tf_op jit(solution)/shard_map/attend/pallas_call | solution.py:186
  70.7 3.5 %all-to-all-start.2 = ((bf16[16,32,128]{2,1,0:T(8,128)(2,1)}), bf16[16,32,128]{2,1,0:T(8,128)(2,1)S(1)}, u32[]{:S(2)}, u32[]{:S(2)}) async-start(bf16[16,32,128]{2,1,0:T(8,128)(2,1)} %attend.1), calls=%async_computation.2 | async-start | bytes 262144 | tf_op jit(solution)/shard_map/all_to_all | solution.py:193
  74.2 0.0 copy-start.1
  74.2 0.6 copy-done.1
  74.9 0.6 subtract_bitcast_fusion.position_ref
  75.4 6.5 %all-to-all-done.2.got_ref = bf16[16,32,128]{2,1,0:T(8,128)(2,1)S(1)} async-done(((bf16[16,32,128]{2,1,0:T(8,128)(2,1)}), bf16[16,32,128]{2,1,0:T(8,128)(2,1)S(1)}, u32[]{:S(2)}, u32[]{:S(2)}) %all-to-all-start.2) | async-done | bytes 131104 | tf_op jit(solution)/shard_map/all_to_all | solution.py:193
  81.9 0.0 copy-start
  81.9 0.7 copy-done
  82.5 2.2 %finish.1 = bf16[128,512]{1,0:T(8,128)(2,1)} custom-call(bf16[16,32,128]{2,1,0:T(8,128)(2,1)} %copy-done, bf16[512,512]{1,0:T(8,128)(2,1)} %wo_ref.1, bf16[128,512]{1,0:T(8,128)(2,1)} %feat_ref.3, s32[1,128]{1,0:T(1,128)} %subtract_bitcast_fusion.position_ref), custom_call_target="tpu_custom_call" | custom-call | tf_op jit(solution)/shard_map/finish/pallas_call | solution.py:197
  84.7 1.0 all_to_all.20
  85.7 22.2 %all_to_all.28 = bf16[64,2,512]{2,1,0:T(2,128)(2,1)S(1)} all-to-all(bf16[64,2,512]{2,1,0:T(2,128)(2,1)S(1)} %all_to_all.20), channel_id=1, replica_groups=mesh['xh'=4,'z'=8,'c'=2,'xl'=2,'y'=8] {'xh','z','c'}, dimensions={0} | all-to-all | bytes 262144 | tf_op jit(solution)/shard_map/all_to_all | solution.py:204
  107.9 0.7 all_to_all.22
Async XLA Ops:
  26.7 31.6 %all-to-all-start.1 = ((bf16[16,64,128]{2,1,0:T(8,128)(2,1)}), bf16[16,64,128]{2,1,0:T(8,128)(2,1)S(1)}, u32[]{:S(2)}, u32[]{:S(2)}) async-start(bf16[16,64,128]{2,1,0:T(8,128)(2,1)} %get-tuple-element.8), calls=%async_computation.1 | async-start | bytes 524288 | tf_op jit(solution)/shard_map/all_to_all | solution.py:183
  70.7 11.2 %all-to-all-start.2 = ((bf16[16,32,128]{2,1,0:T(8,128)(2,1)}), bf16[16,32,128]{2,1,0:T(8,128)(2,1)S(1)}, u32[]{:S(2)}, u32[]{:S(2)}) async-start(bf16[16,32,128]{2,1,0:T(8,128)(2,1)} %attend.1), calls=%async_computation.2 | async-start | bytes 262144 | tf_op jit(solution)/shard_map/all_to_all | solution.py:193
  74.2 0.7 copy-start.1
  81.9 0.7 copy-start

commit v2 on v1

v2 whole, which is shorter than its diff:
```python
import math

import jax
import jax.numpy as jnp
from jax import lax
from jax.experimental import pallas as pl
from jax.experimental.pallas import tpu as pltpu
from jax.sharding import Mesh, PartitionSpec as P

HEADS = 8
BLOCK = 128
HEAD_DIM = 64
HALF = 64
LISTED = 4
PER_DOT = 4
DOTS = 4
UNROLL = 4
LIMIT = 12 << 20
ROWS = 136
SECTORS = 16
GROUP = 16

VMEM = pl.BlockSpec(memory_space=pltpu.VMEM)
SMEM = pl.BlockSpec(memory_space=pltpu.SMEM)
HBM = pl.BlockSpec(memory_space=pltpu.HBM)
PARAMS = pltpu.CompilerParams(vmem_limit_bytes=LIMIT)


def low_lanes(shape):
    return lax.broadcasted_iota(jnp.int32, shape, len(shape) - 1) < HALF


def swap_halves(x):
    return jnp.concatenate([x[:, HALF:], x[:, :HALF]], axis=1)


def pack_kernel(
    feat_hbm, gain_hbm, lat_hbm, wkv_hbm, wq_hbm, list_hbm, len_hbm, dest_hbm, scale_hbm, out_hbm,
    feat_ref, gain_ref, lat_ref, wkv_ref, wq_ref, list_ref, len_ref, dest_ref, scale_ref, row_ref, out_ref, sems, out_sems,
):
    pairs = (
        (feat_hbm, feat_ref), (gain_hbm, gain_ref), (lat_hbm, lat_ref), (wkv_hbm, wkv_ref),
        (wq_hbm, wq_ref), (list_hbm, list_ref), (len_hbm, len_ref), (dest_hbm, dest_ref), (scale_hbm, scale_ref),
    )
    copies = [pltpu.make_async_copy(source, target, sems.at[k]) for k, (source, target) in enumerate(pairs)]
    for copy in copies:
        copy.start()
    for copy in copies[:4]:
        copy.wait()
    values = feat_ref[...].astype(jnp.float32)
    centred = values - jnp.mean(values, axis=-1, keepdims=True)
    spread = jnp.mean(centred * centred, axis=-1, keepdims=True)
    normed = (centred * lax.rsqrt(spread + 1e-05) * gain_ref[...]).astype(jnp.bfloat16)
    for copy in copies[4:]:
        copy.wait()
    queries = jnp.dot(normed, wq_ref[...], preferred_element_type=jnp.float32).astype(jnp.bfloat16)
    lane = lax.broadcasted_iota(jnp.int32, (8, 128), 1)
    row_ref[:, 0:GROUP] = list_ref[...]
    entries = jnp.where(lane < GROUP, jnp.broadcast_to(row_ref[...], (8, 128)), 0)
    entries = jnp.where(lane == GROUP, jnp.broadcast_to(len_ref[...], (8, 128)), entries)
    dest = dest_ref[...]
    position = dest // (BLOCK * SECTORS) * 2 + dest % 2
    row = lax.broadcasted_iota(jnp.int32, (8, 128), 0)
    entries = jnp.where(row == 1, jnp.broadcast_to(position, (8, 128)), entries)
    head_lane = lax.broadcasted_iota(jnp.int32, (1, HEADS), 1)
    own = jnp.where(head_lane == lax.axis_index("y"), scale_ref[...], 0.0)
    own = jnp.broadcast_to(jnp.sum(own, axis=-1, keepdims=True), (8, 128))
    first = own.astype(jnp.bfloat16).astype(jnp.float32)
    second = (own - first).astype(jnp.bfloat16).astype(jnp.float32)
    parts = jnp.where(row == 2, first, jnp.where(row == 3, second, own - first - second))
    entries = jnp.where(row < 2, entries.astype(jnp.float32), parts).astype(jnp.bfloat16)
    low = low_lanes((HALF, 128))
    lat = lat_ref[...]
    swapped = swap_halves(lat)
    sends = []
    for head in range(HEADS):
        tile = slice(head // 2 * 128, head // 2 * 128 + 128)
        key_tile = wkv_ref[:, tile]
        value_tile = wkv_ref[:, slice(tile.start + 512, tile.stop + 512)]
        if head % 2:
            piece = jnp.where(low, swap_halves(key_tile), value_tile)
        else:
            piece = jnp.where(low, key_tile, swap_halves(value_tile))
        for half in range(2):
            query = queries[half * HALF:half * HALF + HALF, tile]
            if head % 2:
                query = swap_halves(query)
            peer = half * HEADS + head
            out_ref[peer, 0:HALF] = jnp.where(low, query, lat if half else swapped)
            out_ref[peer, HALF:2 * HALF] = piece
            out_ref[peer, 2 * HALF:ROWS] = entries
            send = pltpu.make_async_copy(out_ref.at[peer], out_hbm.at[peer], out_sems.at[peer])
            send.start()
            sends.append(send)
    for send in sends:
        send.wait()


def project_kernel(got_ref, out_ref, table_ref, position_ref, scale_ref):
    latent = got_ref[:, 0:HALF, :].reshape(SECTORS * HALF, 128)
    weights = got_ref[:, HALF:2 * HALF, :].reshape(SECTORS * HALF, 128)
    product = lax.dot_general(latent, weights, (((0,), (0,)), ((), ())), preferred_element_type=jnp.float32)
    panel = product[HALF:].astype(jnp.bfloat16)
    for peer in range(out_ref.shape[0]):
        out_ref[peer] = panel
    for source in range(SECTORS):
        row = got_ref[source, 2 * HALF:ROWS, :].astype(jnp.float32).astype(jnp.int32)
        table_ref[source:source + 1] = row[0:1]
    own = got_ref[lax.axis_index(("xl", "y")), 2 * HALF:ROWS, :].astype(jnp.float32)
    position_ref[...] = own[1:2].astype(jnp.int32)
    scale_ref[...] = (own[2:3] + own[3:4]) + own[4:5]


def attend_kernel(table_ref, scale_ref, got_ref, panel_ref, out_ref):
    scale = scale_ref[:, 0:1] * (math.log2(math.e) / math.sqrt(HEAD_DIM))
    contract_last = (((1,), (1,)), ((), ()))

    def finish(source, weighted, denominator):
        attended = (weighted / denominator).astype(jnp.bfloat16)
        upper, lower = attended[0:32], attended[32:64]
        out_ref[source] = jnp.where(low_lanes((32, 128)), swap_halves(upper), lower)

    def query_of(source):
        tile = got_ref[source, 0:HALF]
        return jnp.where(low_lanes((HALF, 128)), tile, jnp.zeros_like(tile))

    dense = table_ref[0, GROUP] > LISTED

    @pl.when(dense)
    def _():
        keys = panel_ref[...].reshape(GROUP * BLOCK, 128)

        def several(first):
            query = jnp.concatenate([query_of(first + k) for k in range(PER_DOT)], axis=0)
            scores = lax.dot_general(query, keys, contract_last, preferred_element_type=jnp.float32)
            weights = jnp.exp2((scores - jnp.max(scores, axis=-1, keepdims=True)) * scale)
            denominator = jnp.sum(weights, axis=-1, keepdims=True)
            weighted = jnp.dot(weights.astype(jnp.bfloat16), keys, preferred_element_type=jnp.float32)
            for k in range(PER_DOT):
                rows = slice(k * HALF, k * HALF + HALF)
                finish(first + k, weighted[rows], denominator[rows])

        @pl.loop(0, SECTORS // (PER_DOT * DOTS))
        def _(step):
            for k in range(DOTS):
                several((step * DOTS + k) * PER_DOT)

    @pl.when(jnp.logical_not(dense))
    def _():
        def one(source):
            query = query_of(source)
            halves = []
            for j in range(LISTED):
                entry = table_ref[source, j]
                core, column = entry % 2, entry // 2
                halves += [panel_ref[core, column], panel_ref[core, HEADS + column]]
            blocks = jnp.concatenate(halves, axis=0)
            scores = lax.dot_general(query, blocks, contract_last, preferred_element_type=jnp.float32)
            column = lax.broadcasted_iota(jnp.int32, scores.shape, 1)
            scores = jnp.where(column < table_ref[source, GROUP] * BLOCK, scores, -jnp.inf)
            weights = jnp.exp2((scores - jnp.max(scores, axis=-1, keepdims=True)) * scale)
            denominator = jnp.sum(weights, axis=-1, keepdims=True)
            weighted = jnp.dot(weights.astype(jnp.bfloat16), blocks, preferred_element_type=jnp.float32)
            finish(source, weighted, denominator)

        @pl.loop(0, SECTORS // UNROLL)
        def _(step):
            for k in range(UNROLL):
                one(step * UNROLL + k)


def finish_kernel(got_ref, wo_ref, feat_ref, position_ref, out_ref):
    low = low_lanes((32, 128))
    rows = []
    for half in range(2):
        upper, lower = [], []
        for pair in range(HEADS // 2):
            even = got_ref[half * HEADS + 2 * pair]
            odd = got_ref[half * HEADS + 2 * pair + 1]
            upper.append(jnp.where(low, even, swap_halves(odd)))
            lower.append(jnp.where(low, swap_halves(even), odd))
        rows += [jnp.concatenate(upper, axis=1), jnp.concatenate(lower, axis=1)]
    attended = jnp.concatenate(rows, axis=0)
    product = jnp.dot(attended, wo_ref[...], preferred_element_type=jnp.float32)
    updated = (feat_ref[...].astype(jnp.float32) + product).astype(jnp.bfloat16)
    slot = lax.broadcasted_iota(jnp.int32, (BLOCK, BLOCK), 0)
    chosen = (slot == position_ref[...]).astype(jnp.float32).astype(jnp.bfloat16)
    moved = jnp.dot(chosen, updated, preferred_element_type=jnp.float32)
    out_ref[...] = moved.reshape(out_ref.shape).astype(jnp.bfloat16)


def shards(grid_feat, latent, query_gain, w_q, w_kv, w_o, head_scale, block_lists, list_len, dest):
    band_axes, sector_axes = ("xh", "z", "c"), ("xl", "y")
    local_rows, width = grid_feat.shape
    bf16 = jnp.bfloat16

    packed = pl.pallas_call(
        pack_kernel,
        out_shape=jax.ShapeDtypeStruct((SECTORS, ROWS, 128), bf16),
        in_specs=[HBM] * 9,
        out_specs=HBM,
        scratch_shapes=[
            pltpu.VMEM((local_rows, width), bf16),
            pltpu.VMEM((1, width), jnp.float32),
            pltpu.VMEM(latent.shape[::-1], bf16),
            pltpu.VMEM(w_kv.shape, bf16),
            pltpu.VMEM(w_q.shape, bf16),
            pltpu.VMEM((1, GROUP), jnp.int32),
            pltpu.VMEM((1, 1), jnp.int32),
            pltpu.VMEM((1, local_rows), jnp.int32),
            pltpu.VMEM((1, HEADS), jnp.float32),
            pltpu.VMEM((1, 128), jnp.int32),
            pltpu.VMEM((SECTORS, ROWS, 128), bf16),
            pltpu.SemaphoreType.DMA((9,)),
            pltpu.SemaphoreType.DMA((SECTORS,)),
        ],
        name="pack",
        compiler_params=pltpu.CompilerParams(vmem_limit_bytes=60 << 20),
    )(
        grid_feat, query_gain.reshape(1, -1), latent.T, w_kv, w_q, block_lists, list_len.reshape(1, 1),
        dest.reshape(1, -1), head_scale.reshape(1, -1),
    )
    got = lax.all_to_all(packed, sector_axes, 0, 0, tiled=True)

    panel, table, position, scale = pl.pallas_call(
        project_kernel,
        out_shape=(
            jax.ShapeDtypeStruct((GROUP, HALF, 128), bf16),
            jax.ShapeDtypeStruct((SECTORS, 128), jnp.int32),
            jax.ShapeDtypeStruct((1, 128), jnp.int32),
            jax.ShapeDtypeStruct((1, 128), jnp.float32),
        ),
        in_specs=[VMEM],
        out_specs=(VMEM,) * 4,
        name="project",
        compiler_params=PARAMS,
    )(got)
    panels = lax.all_to_all(panel, ("xl", "z"), 0, 0, tiled=True)
    panels = lax.all_gather(panels, "c", axis=0)

    attended = pl.pallas_call(
        attend_kernel,
        out_shape=jax.ShapeDtypeStruct((SECTORS, 32, 128), bf16),
        in_specs=[SMEM, VMEM, VMEM, VMEM],
        out_specs=VMEM,
        name="attend",
        compiler_params=PARAMS,
    )(table, scale, got, panels)
    attended = lax.all_to_all(attended, sector_axes, 0, 0, tiled=True)

    outgoing = pl.pallas_call(
        finish_kernel,
        out_shape=jax.ShapeDtypeStruct((local_rows // 2, 2, width), bf16),
        in_specs=[VMEM, VMEM, VMEM, VMEM],
        out_specs=VMEM,
        name="finish",
        compiler_params=PARAMS,
    )(attended, w_o, grid_feat, position)
    arrived = lax.all_to_all(outgoing, band_axes, 0, 0, tiled=True)
    return arrived.reshape(local_rows, width)


def solution(mesh):
    fine = Mesh(mesh.devices.reshape(4, 8, 2, 2, 8), ("xh", "z", "c", "xl", "y"))
    band, sector = ("xh", "z", "c"), ("xl", "y")
    return jax.shard_map(
        shards,
        mesh=fine,
        in_specs=(
            P(band + sector, None),
            P(band, sector),
            P(),
            P(),
            P(sector, None),
            P(),
            P(),
            P(band + sector, None),
            P(band + sector),
            P(band + sector),
        ),
        out_specs=P(band + sector, None),
        check_vma=False,
    )
```

time: 109 us -> 101 us (0.927)
  blocking collectives: 48.5 us -> 90.6 us
  starting transfers between devices: 26.9 us -> 0 us
  waiting for transfers between devices: 14.6 us -> 0 us
  Pallas kernels: 14.3 us -> 9.01 us
  local copies, waits for them, and re-layouts: 2.98 us -> 0.72 us
    all_to_all x1 -> x3, blocking collectives: 22.2 us -> 64.5 us  [the longest x1 31.4 us: shards(): panels = lax.all_to_all(panel, ('xl', 'z'), 0, 0, tiled=True)]
    all_to_all x2 -> x0, starting transfers between devices: 26.9 us -> none  [the longest x1 23.4 us: shards(): panels = lax.all_to_all(panel, ('xl', 'z'), 0, 0, tiled=True)]
    all_to_all x2 -> x0, waiting for transfers between devices: 14.6 us -> none  [the longest x1 8.15 us: shards(): panels = lax.all_to_all(panel, ('xl', 'z'), 0, 0, tiled=True)]
    pallas_call x1, Pallas kernels: 7.65 us -> 5.69 us  [shards(): pl.pallas_call(attend_kernel, out_shape=jax.ShapeDtypeStruct((SECTORS, 32...]
    pallas_call x1, Pallas kernels: 2.05 us -> 0.27 us  [shards(): pl.pallas_call(project_kernel, out_shape=(jax.ShapeDtypeStruct((GROUP, HA...]
    all_to_all x2 -> x0, local copies, waits for them, and re-layouts: 1.67 us -> none  [shards(): return lax.all_to_all(outgoing, band_axes, 0, 0, tiled=True)]
    pallas_call x1, Pallas kernels: 2.18 us -> 0.52 us  [shards(): pl.pallas_call(finish_kernel, out_shape=jax.ShapeDtypeStruct((local_rows...]
    unnamed x4, local copies, waits for them, and re-layouts: 1.3 us -> 0.01 us
  transfers between devices with their start and end apart: 2 -> 0, of which waited for: 2 -> 0; matrix products, arithmetic and copies ran while one was open for 1% -> 0% of each run, Pallas kernels for 0% -> 0%
where the time goes in v2:
time: 101 us
  blocking collectives  90.6 us (90%)
  Pallas kernels  9.01 us (9%)
    all_to_all x1, blocking collectives, shards(): panels = lax.all_to_all(panel, ('xl', 'z'), 0, 0, tiled=True)  31.4 us
    all_to_all x1, blocking collectives, shards(): arrived = lax.all_to_all(outgoing, band_axes, 0, 0, tiled=True)  22.7 us
    all_to_all x1, blocking collectives, shards(): got = lax.all_to_all(packed, sector_axes, 0, 0, tiled=True)  21.5 us
    all_to_all x1, blocking collectives, shards(): attended = lax.all_to_all(attended, sector_axes, 0, 0, tiled=True)  10.4 us
    pallas_call x1, Pallas kernels, shards(): pl.pallas_call(attend_kernel, out_shape=jax.ShapeDtypeStruct((SECTORS, 32...  5.69 us
    all_gather x1, blocking collectives, shards(): panels = lax.all_gather(panels, 'c', axis=0)  4.6 us
    pallas_call x1, Pallas kernels, shards(): pl.pallas_call(pack_kernel, out_shape=jax.ShapeDtypeStruct((SECTORS, ROWS...  2.53 us

profile of v2, /device:TPU:1, one launch (start us, length us, event | category | flops | bytes accessed | tf_op | source)
XLA Modules:
  0.0 101.0 jit_solution(13604087028820028962)
XLA Ops:
  0.7 2.5 %pack.1 = bf16[16,136,128]{2,1,0:T(8,128)(2,1)} custom-call(bf16[128,512]{1,0:T(8,128)(2,1)} %feat_ref.1, f32[1,512]{1,0:T(1,128)} %bitcast.9, bf16[64,128]{1,0:T(8,128)(2,1)} %bitcast.8, bf16[64,1024]{1,0:T(8,128)(2,1)} %wkv_hbm.1, bf16[512,512]{1,0:T(8,128)(2,1)} %wq_hbm.1, s32[1,16]{1,0:T(1,128)} %list_hbm.1, s32[1,1]{1,0:T(1,128)} %bitcast.6.len_hbm, ...), custom_call_target="tpu_custom_call" | custom-call | tf_op jit(solution)/shard_map/pack/pallas_call | solution.py:197
  3.2 21.5 %all_to_all.20.got_ref = bf16[16,136,128]{2,1,0:T(8,128)(2,1)S(1)} all-to-all(bf16[16,136,128]{2,1,0:T(8,128)(2,1)} %pack.1), channel_id=1, replica_groups=mesh['xh'=4,'z'=8,'c'=2,'xl'=2,'y'=8] {'xl','y'}, dimensions={0} | all-to-all | bytes 1114112 | tf_op jit(solution)/shard_map/all_to_all | solution.py:223
  24.7 0.3 project.1
  24.9 31.4 %all_to_all.21 = bf16[16,64,128]{2,1,0:T(8,128)(2,1)S(1)} all-to-all(bf16[16,64,128]{2,1,0:T(8,128)(2,1)S(1)} %get-tuple-element.11), channel_id=1, replica_groups=mesh['xh'=4,'z'=8,'c'=2,'xl'=2,'y'=8] {'xl','z'}, dimensions={0} | all-to-all | bytes 524288 | tf_op jit(solution)/shard_map/all_to_all | solution.py:238
  56.3 4.6 %all-gather = bf16[32,64,128]{2,1,0:T(8,128)(2,1)S(1)} all-gather(bf16[16,64,128]{2,1,0:T(8,128)(2,1)S(1)} %all_to_all.21), channel_id=2, replica_groups=mesh['xh'=4,'z'=8,'c'=2,'xl'=2,'y'=8] {'c'}, dimensions={0}, use_global_device_ids=true | all-gather | bytes 786432 | tf_op jit(solution)/shard_map/all_gather | solution.py:239
  60.9 0.0 copy-start
  60.9 5.7 %attend.1 = bf16[16,32,128]{2,1,0:T(8,128)(2,1)S(1)} custom-call(s32[16,128]{1,0:T(8,128)S(1)} %get-tuple-element.9.table_ref, f32[1,128]{1,0:T(1,128)S(1)} %get-tuple-element.10.scale_ref, bf16[16,136,128]{2,1,0:T(8,128)(2,1)S(1)} %all_to_all.20.got_ref, bf16[2,16,64,128]{3,2,1,0:T(8,128)(2,1)S(1)} %bitcast.7), custom_call_target="tpu_custom_call" | custom-call | tf_op jit(solution)/shard_map/attend/pallas_call | solution.py:241
  66.6 0.0 copy-start.1
  66.6 10.4 %all_to_all.22.got_ref = bf16[16,32,128]{2,1,0:T(8,128)(2,1)S(1)} all-to-all(bf16[16,32,128]{2,1,0:T(8,128)(2,1)S(1)} %attend.1), channel_id=1, replica_groups=mesh['xh'=4,'z'=8,'c'=2,'xl'=2,'y'=8] {'xl','y'}, dimensions={0} | all-to-all | bytes 262144 | tf_op jit(solution)/shard_map/all_to_all | solution.py:249
  77.0 0.0 copy-done
  77.0 0.0 copy-done.1
  77.0 0.5 finish.1
  77.6 22.7 %all_to_all.23 = bf16[64,2,512]{2,1,0:T(2,128)(2,1)S(1)} all-to-all(bf16[64,2,512]{2,1,0:T(2,128)(2,1)S(1)} %finish.1), channel_id=1, replica_groups=mesh['xh'=4,'z'=8,'c'=2,'xl'=2,'y'=8] {'xh','z','c'}, dimensions={0} | all-to-all | bytes 262144 | tf_op jit(solution)/shard_map/all_to_all | solution.py:259
  100.3 0.7 reshape.19
Async XLA Ops:
  60.9 16.1 %copy-start = (bf16[512,512]{1,0:T(8,128)(2,1)S(1)}, bf16[512,512]{1,0:T(8,128)(2,1)}, u32[]{:S(2)}) copy-start(bf16[512,512]{1,0:T(8,128)(2,1)} %wo_ref.1) | copy-start | bytes 1572868
  66.6 10.4 %copy-start.1 = (bf16[128,512]{1,0:T(8,128)(2,1)S(1)}, bf16[128,512]{1,0:T(8,128)(2,1)}, u32[]{:S(2)}) copy-start(bf16[128,512]{1,0:T(8,128)(2,1)} %feat_ref.1) | copy-start | bytes 393220

commit v3 on v2

v3 whole, which is shorter than its diff:
```python
import math

import jax
import jax.numpy as jnp
from jax import lax
from jax.experimental import pallas as pl
from jax.experimental.pallas import tpu as pltpu
from jax.sharding import Mesh, PartitionSpec as P

HEADS = 8
BLOCK = 128
HEAD_DIM = 64
HALF = 64
LISTED = 4
GROUP = 16
SECTORS = 16
SOURCES = 8
ROWS = 200
TAIL = 3 * HALF
PER_DOT = 2

VMEM = pl.BlockSpec(memory_space=pltpu.VMEM)
SMEM = pl.BlockSpec(memory_space=pltpu.SMEM)
HBM = pl.BlockSpec(memory_space=pltpu.HBM)
PARAMS = pltpu.CompilerParams(vmem_limit_bytes=12 << 20)
CONTRACT_LAST = (((1,), (1,)), ((), ()))
CONTRACT_FIRST = (((0,), (0,)), ((), ()))


def low_lanes(rows):
    return lax.broadcasted_iota(jnp.int32, (rows, 128), 1) < HALF


def swap_halves(x):
    return jnp.concatenate([x[:, HALF:], x[:, :HALF]], axis=1)


def pack_kernel(
    feat_hbm, gain_hbm, lat_hbm, wkv_hbm, wq_hbm, list_hbm, len_hbm, dest_hbm, scale_hbm, out_hbm,
    feat_ref, gain_ref, lat_ref, wkv_ref, wq_ref, list_ref, len_ref, dest_ref, scale_ref, row_ref, out_ref,
    sems, out_sems,
):
    pairs = (
        (feat_hbm, feat_ref), (gain_hbm, gain_ref), (lat_hbm, lat_ref), (wkv_hbm, wkv_ref),
        (wq_hbm, wq_ref), (list_hbm, list_ref), (len_hbm, len_ref), (dest_hbm, dest_ref), (scale_hbm, scale_ref),
    )
    copies = [pltpu.make_async_copy(source, target, sems.at[k]) for k, (source, target) in enumerate(pairs)]
    for copy in copies:
        copy.start()
    for copy in copies[:4]:
        copy.wait()
    values = feat_ref[...].astype(jnp.float32)
    centred = values - jnp.mean(values, axis=-1, keepdims=True)
    spread = jnp.mean(centred * centred, axis=-1, keepdims=True)
    normed = (centred * lax.rsqrt(spread + 1e-05) * gain_ref[...]).astype(jnp.bfloat16)
    for copy in copies[4:]:
        copy.wait()
    queries = jnp.dot(normed, wq_ref[...], preferred_element_type=jnp.float32).astype(jnp.bfloat16)
    lane = lax.broadcasted_iota(jnp.int32, (8, 128), 1)
    row = lax.broadcasted_iota(jnp.int32, (8, 128), 0)
    row_ref[:, 0:GROUP] = list_ref[...]
    entries = jnp.where(lane < GROUP, jnp.broadcast_to(row_ref[...], (8, 128)), 0)
    entries = jnp.where(lane == GROUP, jnp.broadcast_to(len_ref[...], (8, 128)), entries)
    dest = dest_ref[...]
    position = dest // (BLOCK * SECTORS) * 2 + dest % 2
    entries = jnp.where(row == 1, jnp.broadcast_to(position, (8, 128)), entries)
    head_lane = lax.broadcasted_iota(jnp.int32, (1, HEADS), 1)
    own = jnp.where(head_lane == lax.axis_index("y"), scale_ref[...], 0.0)
    own = jnp.broadcast_to(jnp.sum(own, axis=-1, keepdims=True), (8, 128))
    first = own.astype(jnp.bfloat16).astype(jnp.float32)
    second = (own - first).astype(jnp.bfloat16).astype(jnp.float32)
    parts = jnp.where(row == 2, first, jnp.where(row == 3, second, own - first - second))
    entries = jnp.where(row < 2, entries.astype(jnp.float32), parts).astype(jnp.bfloat16)
    low = low_lanes(HALF)
    sends = []
    for head in range(HEADS):
        tile = slice(head // 2 * 128, head // 2 * 128 + 128)
        keys = wkv_ref[:, tile]
        values = wkv_ref[:, slice(tile.start + 512, tile.stop + 512)]
        upper, lower = queries[0:HALF, tile], queries[HALF:BLOCK, tile]
        if head % 2:
            keys, upper = swap_halves(keys), swap_halves(upper)
        else:
            values, lower = swap_halves(values), swap_halves(lower)
        out_ref[head, 0:HALF] = lat_ref[...]
        out_ref[head, HALF:2 * HALF] = jnp.where(low, keys, values)
        out_ref[head, 2 * HALF:TAIL] = jnp.where(low, upper, lower)
        out_ref[head, TAIL:ROWS] = entries
        send = pltpu.make_async_copy(out_ref.at[head], out_hbm.at[head], out_sems.at[head])
        send.start()
        sends.append(send)
    for send in sends:
        send.wait()


def project_kernel(got_ref, out_ref, table_ref, position_ref, scale_ref):
    latent = got_ref[:, 0:HALF, :].reshape(SOURCES * HALF, 128)
    weights = got_ref[:, HALF:2 * HALF, :].reshape(SOURCES * HALF, 128)
    out_ref[...] = lax.dot_general(latent, weights, CONTRACT_FIRST, preferred_element_type=jnp.float32)
    lane = lax.broadcasted_iota(jnp.int32, (8, 128), 1)
    for source in range(SOURCES):
        row = got_ref[source, TAIL:ROWS, :].astype(jnp.float32).astype(jnp.int32)
        slots = jnp.bitwise_and(row, 1) * (GROUP // 2) + jnp.right_shift(row, 1)
        table_ref[source:source + 1] = jnp.where(lane == GROUP, row * BLOCK, slots)[0:1]
    own = got_ref[lax.axis_index("y"), TAIL:ROWS, :].astype(jnp.float32)
    position_ref[...] = own[1:2].astype(jnp.int32)
    scale_ref[...] = (own[2:3] + own[3:4]) + own[4:5]


def join_kernel(parts_ref, out_ref):
    panel = (parts_ref[0] + parts_ref[1]).astype(jnp.bfloat16)
    for peer in range(out_ref.shape[0]):
        out_ref[peer] = panel


def attend_kernel(table_ref, scale_ref, got_ref, panel_ref, out_ref, query_ref, score_ref, prob_ref, total_ref):
    scale = scale_ref[:, 0:1] * (math.log2(math.e) / math.sqrt(HEAD_DIM))
    low = low_lanes(HALF)
    for source in range(SOURCES):
        tile = got_ref[source, 2 * HALF:TAIL]
        zero = jnp.zeros_like(tile)
        query_ref[source * BLOCK:source * BLOCK + HALF] = jnp.where(low, tile, zero)
        query_ref[source * BLOCK + HALF:source * BLOCK + BLOCK] = jnp.where(low, swap_halves(tile), zero)

    def finish(source, weighted, denominator):
        attended = (weighted / denominator).astype(jnp.bfloat16)
        out_ref[source] = jnp.where(low, swap_halves(attended[0:HALF]), attended[HALF:BLOCK])

    def blocks_of(source):
        return jnp.concatenate([panel_ref[table_ref[source, j]] for j in range(LISTED)], axis=0)

    dense = table_ref[0, GROUP] > LISTED * BLOCK

    @pl.when(jnp.logical_not(dense))
    def _():
        for source in range(SOURCES):
            rows = slice(source * BLOCK, source * BLOCK + BLOCK)
            score = lax.dot_general(
                query_ref[rows], blocks_of(source), CONTRACT_LAST, preferred_element_type=jnp.float32
            )
            column = lax.broadcasted_iota(jnp.int32, score.shape, 1)
            score_ref[rows] = jnp.where(column < table_ref[source, GROUP], score, -jnp.inf)
        scores = score_ref[...]
        weights = jnp.exp2((scores - jnp.max(scores, axis=-1, keepdims=True)) * scale)
        total_ref[...] = jnp.broadcast_to(jnp.sum(weights, axis=-1, keepdims=True), total_ref.shape)
        prob_ref[...] = weights.astype(jnp.bfloat16)
        for source in range(SOURCES):
            rows = slice(source * BLOCK, source * BLOCK + BLOCK)
            weighted = jnp.dot(prob_ref[rows], blocks_of(source), preferred_element_type=jnp.float32)
            finish(source, weighted, total_ref[rows])

    @pl.when(dense)
    def _():
        keys = panel_ref[...].reshape(GROUP * BLOCK, 128)
        for first in range(0, SOURCES, PER_DOT):
            query = query_ref[first * BLOCK:(first + PER_DOT) * BLOCK]
            scores = lax.dot_general(query, keys, CONTRACT_LAST, preferred_element_type=jnp.float32)
            weights = jnp.exp2((scores - jnp.max(scores, axis=-1, keepdims=True)) * scale)
            total = jnp.sum(weights, axis=-1, keepdims=True)
            weighted = jnp.dot(weights.astype(jnp.bfloat16), keys, preferred_element_type=jnp.float32)
            for k in range(PER_DOT):
                rows = slice(k * BLOCK, k * BLOCK + BLOCK)
                finish(first + k, weighted[rows], total[rows])


def finish_kernel(got_ref, wo_ref, feat_ref, position_ref, out_ref):
    low = low_lanes(HALF)
    upper, lower = [], []
    for pair in range(HEADS // 2):
        even, odd = got_ref[2 * pair], got_ref[2 * pair + 1]
        upper.append(jnp.where(low, even, swap_halves(odd)))
        lower.append(jnp.where(low, swap_halves(even), odd))
    attended = jnp.concatenate([jnp.concatenate(upper, axis=1), jnp.concatenate(lower, axis=1)], axis=0)
    product = jnp.dot(attended, wo_ref[...], preferred_element_type=jnp.float32)
    updated = (feat_ref[...].astype(jnp.float32) + product).astype(jnp.bfloat16)
    slot = lax.broadcasted_iota(jnp.int32, (BLOCK, BLOCK), 0)
    chosen = (slot == position_ref[...]).astype(jnp.float32).astype(jnp.bfloat16)
    moved = jnp.dot(chosen, updated, preferred_element_type=jnp.float32)
    out_ref[...] = moved.reshape(out_ref.shape).astype(jnp.bfloat16)


def shards(grid_feat, latent, query_gain, w_q, w_kv, w_o, head_scale, block_lists, list_len, dest):
    local_rows, width = grid_feat.shape
    bf16, f32, i32 = jnp.bfloat16, jnp.float32, jnp.int32
    shaped = jax.ShapeDtypeStruct

    packed = pl.pallas_call(
        pack_kernel,
        out_shape=shaped((HEADS, ROWS, 128), bf16),
        in_specs=[HBM] * 9,
        out_specs=HBM,
        scratch_shapes=[
            pltpu.VMEM((local_rows, width), bf16),
            pltpu.VMEM((1, width), f32),
            pltpu.VMEM(latent.shape[::-1], bf16),
            pltpu.VMEM(w_kv.shape, bf16),
            pltpu.VMEM(w_q.shape, bf16),
            pltpu.VMEM((1, GROUP), i32),
            pltpu.VMEM((1, 1), i32),
            pltpu.VMEM((1, local_rows), i32),
            pltpu.VMEM((1, HEADS), f32),
            pltpu.VMEM((1, 128), i32),
            pltpu.VMEM((HEADS, ROWS, 128), bf16),
            pltpu.SemaphoreType.DMA((9,)),
            pltpu.SemaphoreType.DMA((HEADS,)),
        ],
        name="pack",
        compiler_params=pltpu.CompilerParams(vmem_limit_bytes=60 << 20),
    )(
        grid_feat, query_gain.reshape(1, -1), latent.T, w_kv, w_q, block_lists, list_len.reshape(1, 1),
        dest.reshape(1, -1), head_scale.reshape(1, -1),
    )
    got = lax.all_to_all(packed, "y", 0, 0, tiled=True)

    partial, table, position, scale = pl.pallas_call(
        project_kernel,
        out_shape=(
            shaped((BLOCK, 128), f32), shaped((SOURCES, 128), i32), shaped((1, 128), i32), shaped((1, 128), f32)
        ),
        in_specs=[VMEM],
        out_specs=(VMEM,) * 4,
        name="project",
        compiler_params=PARAMS,
    )(got)
    parts = lax.all_gather(partial, "xl", axis=0)
    panel = pl.pallas_call(
        join_kernel,
        out_shape=shaped((GROUP // 2, BLOCK, 128), bf16),
        in_specs=[VMEM],
        out_specs=VMEM,
        name="join",
        compiler_params=PARAMS,
    )(parts)
    panels = lax.all_to_all(panel, "z", 0, 0, tiled=True)
    panels = lax.all_gather(panels, "c", axis=0).reshape(GROUP, BLOCK, 128)

    attended = pl.pallas_call(
        attend_kernel,
        out_shape=shaped((SOURCES, HALF, 128), bf16),
        in_specs=[SMEM, VMEM, VMEM, VMEM],
        out_specs=VMEM,
        scratch_shapes=[
            pltpu.VMEM((SOURCES * BLOCK, 128), bf16),
            pltpu.VMEM((SOURCES * BLOCK, LISTED * BLOCK), f32),
            pltpu.VMEM((SOURCES * BLOCK, LISTED * BLOCK), bf16),
            pltpu.VMEM((SOURCES * BLOCK, 128), f32),
        ],
        name="attend",
        compiler_params=PARAMS,
    )(table, scale, got, panels)
    attended = lax.all_to_all(attended, "y", 0, 0, tiled=True)

    outgoing = pl.pallas_call(
        finish_kernel,
        out_shape=shaped((local_rows // 2, 2, width), bf16),
        in_specs=[VMEM] * 4,
        out_specs=VMEM,
        name="finish",
        compiler_params=PARAMS,
    )(attended, w_o, grid_feat, position)
    arrived = lax.all_to_all(outgoing, ("xh", "z", "c"), 0, 0, tiled=True)
    return arrived.reshape(local_rows, width)


def solution(mesh):
    fine = Mesh(mesh.devices.reshape(4, 8, 2, 2, 8), ("xh", "z", "c", "xl", "y"))
    band, sector = ("xh", "z", "c"), ("xl", "y")
    return jax.shard_map(
        shards,
        mesh=fine,
        in_specs=(
            P(band + sector, None),
            P(band, sector),
            P(),
            P(),
            P(sector, None),
            P(),
            P(),
            P(band + sector, None),
            P(band + sector),
            P(band + sector),
        ),
        out_specs=P(band + sector, None),
        check_vma=False,
    )
```

time: 101 us -> 96.9 us (0.959)
  Pallas kernels: 9.01 us -> 4.92 us
    all_to_all x4, blocking collectives: 86 us -> 77 us  [the longest x1 25.7 us: shards(): panels = lax.all_to_all(panel, 'z', 0, 0, tiled=True)]
    all_gather x1 -> x2, blocking collectives: 4.6 us -> 13.2 us  [the longest x1 6.61 us: shards(): panels = lax.all_gather(panels, 'c', axis=0).reshape(GROUP, BLOCK, 128)]
    pallas_call x4 -> x5, Pallas kernels: 9.01 us -> 4.92 us  [the longest x1 2.44 us: shards(): pl.pallas_call(pack_kernel, out_shape=shaped((HEADS, ROWS, 128), bf16), i...]
where the time goes in v3:
time: 96.9 us; the launch traced here: 96.5 us
  blocking collectives  90.2 us (93%)
  Pallas kernels  4.92 us (5%)
    all_to_all x1, blocking collectives, shards(): panels = lax.all_to_all(panel, 'z', 0, 0, tiled=True)  25.7 us
    all_to_all x1, blocking collectives, shards(): arrived = lax.all_to_all(outgoing, ('xh', 'z', 'c'), 0, 0, tiled=True)  21.9 us
    all_to_all x1, blocking collectives, shards(): got = lax.all_to_all(packed, 'y', 0, 0, tiled=True)  19 us
    all_to_all x1, blocking collectives, shards(): attended = lax.all_to_all(attended, 'y', 0, 0, tiled=True)  10.4 us
    all_gather x1, blocking collectives, shards(): panels = lax.all_gather(panels, 'c', axis=0).reshape(GROUP, BLOCK, 128)  6.61 us
    all_gather x1, blocking collectives, shards(): parts = lax.all_gather(partial, 'xl', axis=0)  6.57 us
    pallas_call x1, Pallas kernels, shards(): pl.pallas_call(pack_kernel, out_shape=shaped((HEADS, ROWS, 128), bf16), i...  2.44 us

profile of v3, /device:TPU:1, one launch (start us, length us, event | category | flops | bytes accessed | tf_op | source)
XLA Modules:
  0.0 96.5 jit_solution(14271032614119384504)
XLA Ops:
  0.7 2.4 %pack.1 = bf16[8,200,128]{2,1,0:T(8,128)(2,1)} custom-call(bf16[128,512]{1,0:T(8,128)(2,1)} %feat_ref.1, f32[1,512]{1,0:T(1,128)} %bitcast.9, bf16[64,128]{1,0:T(8,128)(2,1)} %bitcast.8, bf16[64,1024]{1,0:T(8,128)(2,1)} %wkv_hbm.1, bf16[512,512]{1,0:T(8,128)(2,1)} %wq_hbm.1, s32[1,16]{1,0:T(1,128)} %list_hbm.1, s32[1,1]{1,0:T(1,128)} %bitcast.6.len_hbm, ...), custom_call_target="tpu_custom_call" | custom-call | tf_op jit(solution)/shard_map/pack/pallas_call | solution.py:187
  3.1 19.0 %all_to_all.20.got_ref = bf16[8,200,128]{2,1,0:T(8,128)(2,1)S(1)} all-to-all(bf16[8,200,128]{2,1,0:T(8,128)(2,1)} %pack.1), channel_id=1, replica_groups=mesh['xh'=4,'z'=8,'c'=2,'xl'=2,'y'=8] {'y'}, dimensions={0} | all-to-all | bytes 819200 | tf_op jit(solution)/shard_map/all_to_all | solution.py:213
  22.1 0.2 project.1
  22.3 6.6 %all-gather = f32[256,128]{1,0:T(8,128)S(1)} all-gather(f32[128,128]{1,0:T(8,128)S(1)} %get-tuple-element.11), channel_id=2, replica_groups=mesh['xh'=4,'z'=8,'c'=2,'xl'=2,'y'=8] {'xl'}, dimensions={0}, use_global_device_ids=true | all-gather | bytes 196608 | tf_op jit(solution)/shard_map/all_gather | solution.py:225
  28.9 25.7 %all_to_all.21 = bf16[8,128,128]{2,1,0:T(8,128)(2,1)S(1)} all-to-all(bf16[8,128,128]{2,1,0:T(8,128)(2,1)S(1)} %join.1), channel_id=1, replica_groups=mesh['xh'=4,'z'=8,'c'=2,'xl'=2,'y'=8] {'z'}, dimensions={0} | all-to-all | bytes 524288 | tf_op jit(solution)/shard_map/all_to_all | solution.py:234
  54.6 6.6 %all-gather.1.panel_ref = bf16[16,128,128]{2,1,0:T(8,128)(2,1)S(1)} all-gather(bf16[8,128,128]{2,1,0:T(8,128)(2,1)S(1)} %all_to_all.21), channel_id=3, replica_groups=mesh['xh'=4,'z'=8,'c'=2,'xl'=2,'y'=8] {'c'}, dimensions={0}, use_global_device_ids=true | all-gather | bytes 786432 | tf_op jit(solution)/shard_map/all_gather | solution.py:235
  61.2 0.0 copy-start.1
  61.2 1.7 %attend.1 = bf16[8,64,128]{2,1,0:T(8,128)(2,1)S(1)} custom-call(s32[8,128]{1,0:T(8,128)S(1)} %get-tuple-element.9.table_ref, f32[1,128]{1,0:T(1,128)S(1)} %get-tuple-element.10.scale_ref, bf16[8,200,128]{2,1,0:T(8,128)(2,1)S(1)} %all_to_all.20.got_ref, bf16[16,128,128]{2,1,0:T(8,128)(2,1)S(1)} %all-gather.1.panel_ref), custom_call_target="tpu_custom_call" | custom-call | tf_op jit(solution)/shard_map/attend/pallas_call | solution.py:237
  63.0 0.0 copy-start
  63.0 10.4 %all_to_all.22.got_ref = bf16[8,64,128]{2,1,0:T(8,128)(2,1)S(1)} all-to-all(bf16[8,64,128]{2,1,0:T(8,128)(2,1)S(1)} %attend.1), channel_id=1, replica_groups=mesh['xh'=4,'z'=8,'c'=2,'xl'=2,'y'=8] {'y'}, dimensions={0} | all-to-all | bytes 262144 | tf_op jit(solution)/shard_map/all_to_all | solution.py:251
  73.4 0.0 copy-done.1
  73.4 0.0 copy-done
  73.4 0.5 finish.1
  74.0 21.9 %all_to_all.23 = bf16[64,2,512]{2,1,0:T(2,128)(2,1)S(1)} all-to-all(bf16[64,2,512]{2,1,0:T(2,128)(2,1)S(1)} %finish.1), channel_id=1, replica_groups=mesh['xh'=4,'z'=8,'c'=2,'xl'=2,'y'=8] {'xh','z','c'}, dimensions={0} | all-to-all | bytes 262144 | tf_op jit(solution)/shard_map/all_to_all | solution.py:261
  95.8 0.7 reshape.23
  (1 shorter events, 0.0 us)
Async XLA Ops:
  61.2 12.2 %copy-start.1 = (bf16[512,512]{1,0:T(8,128)(2,1)S(1)}, bf16[512,512]{1,0:T(8,128)(2,1)}, u32[]{:S(2)}) copy-start(bf16[512,512]{1,0:T(8,128)(2,1)} %wo_ref.1) | copy-start | bytes 1572868
  63.0 10.5 %copy-start = (bf16[128,512]{1,0:T(8,128)(2,1)S(1)}, bf16[128,512]{1,0:T(8,128)(2,1)}, u32[]{:S(2)}) copy-start(bf16[128,512]{1,0:T(8,128)(2,1)} %feat_ref.1) | copy-start | bytes 393220

commit v4 on v3

--- a/solution.py
+++ b/solution.py
@@ -17,12 +17,12 @@
 SOURCES = 8
 ROWS = 200
 TAIL = 3 * HALF
-PER_DOT = 2
+PER_DOT = 4
 
 VMEM = pl.BlockSpec(memory_space=pltpu.VMEM)
 SMEM = pl.BlockSpec(memory_space=pltpu.SMEM)
 HBM = pl.BlockSpec(memory_space=pltpu.HBM)
-PARAMS = pltpu.CompilerParams(vmem_limit_bytes=12 << 20)
+PARAMS = pltpu.CompilerParams(vmem_limit_bytes=24 << 20)
 CONTRACT_LAST = (((1,), (1,)), ((), ()))
 CONTRACT_FIRST = (((0,), (0,)), ((), ()))
 
@@ -36,9 +36,8 @@
 
 
 def pack_kernel(
-    feat_hbm, gain_hbm, lat_hbm, wkv_hbm, wq_hbm, list_hbm, len_hbm, dest_hbm, scale_hbm, out_hbm,
-    feat_ref, gain_ref, lat_ref, wkv_ref, wq_ref, list_ref, len_ref, dest_ref, scale_ref, row_ref, out_ref,
-    sems, out_sems,
+    feat_hbm, gain_hbm, lat_hbm, wkv_hbm, wq_hbm, list_hbm, len_hbm, dest_hbm, scale_hbm, out_ref,
+    feat_ref, gain_ref, lat_ref, wkv_ref, wq_ref, list_ref, len_ref, dest_ref, scale_ref, row_ref, sems,
 ):
     pairs = (
         (feat_hbm, feat_ref), (gain_hbm, gain_ref), (lat_hbm, lat_ref), (wkv_hbm, wkv_ref),
@@ -72,7 +71,6 @@
     parts = jnp.where(row == 2, first, jnp.where(row == 3, second, own - first - second))
     entries = jnp.where(row < 2, entries.astype(jnp.float32), parts).astype(jnp.bfloat16)
     low = low_lanes(HALF)
-    sends = []
     for head in range(HEADS):
         tile = slice(head // 2 * 128, head // 2 * 128 + 128)
         keys = wkv_ref[:, tile]
@@ -86,11 +84,6 @@
         out_ref[head, HALF:2 * HALF] = jnp.where(low, keys, values)
         out_ref[head, 2 * HALF:TAIL] = jnp.where(low, upper, lower)
         out_ref[head, TAIL:ROWS] = entries
-        send = pltpu.make_async_copy(out_ref.at[head], out_hbm.at[head], out_sems.at[head])
-        send.start()
-        sends.append(send)
-    for send in sends:
-        send.wait()
 
 
 def project_kernel(got_ref, out_ref, table_ref, position_ref, scale_ref):
@@ -113,7 +106,7 @@
         out_ref[peer] = panel
 
 
-def attend_kernel(table_ref, scale_ref, got_ref, panel_ref, out_ref, query_ref, score_ref, prob_ref, total_ref):
+def attend_kernel(table_ref, scale_ref, got_ref, panel_ref, out_ref, query_ref, score_ref, prob_ref, total_ref, values_ref, full_ref):
     scale = scale_ref[:, 0:1] * (math.log2(math.e) / math.sqrt(HEAD_DIM))
     low = low_lanes(HALF)
     for source in range(SOURCES):
@@ -152,15 +145,33 @@
     @pl.when(dense)
     def _():
         keys = panel_ref[...].reshape(GROUP * BLOCK, 128)
+        span = PER_DOT * BLOCK
+
+        def score(first):
+            query = query_ref[first * BLOCK:first * BLOCK + span]
+            full_ref[:, first * BLOCK:first * BLOCK + span] = lax.dot_general(
+                keys, query, CONTRACT_LAST, preferred_element_type=jnp.float32
+            )
+
+        def rest(first):
+            scores = full_ref[:, first * BLOCK:first * BLOCK + span]
+            weights = jnp.exp2((scores - jnp.max(scores, axis=0, keepdims=True)) * scale)
+            total = jnp.sum(weights, axis=0, keepdims=True)
+            weighted = jnp.dot(values_ref[...], weights.astype(jnp.bfloat16), preferred_element_type=jnp.float32)
+            attended = weighted / total
+            for k in range(PER_DOT):
+                piece = attended[:, k * BLOCK:k * BLOCK + BLOCK]
+                piece = jnp.transpose(jnp.concatenate([piece, swap_halves(piece)], axis=0))
+                out_ref[first + k] = piece[0:HALF].astype(jnp.bfloat16)
+
+        score(0)
+        for block in range(GROUP):
+            turned = jnp.transpose(panel_ref[block].astype(jnp.float32))
+            values_ref[:, block * BLOCK:block * BLOCK + BLOCK] = turned[HALF:BLOCK].astype(jnp.bfloat16)
         for first in range(0, SOURCES, PER_DOT):
-            query = query_ref[first * BLOCK:(first + PER_DOT) * BLOCK]
-            scores = lax.dot_general(query, keys, CONTRACT_LAST, preferred_element_type=jnp.float32)
-            weights = jnp.exp2((scores - jnp.max(scores, axis=-1, keepdims=True)) * scale)
-            total = jnp.sum(weights, axis=-1, keepdims=True)
-            weighted = jnp.dot(weights.astype(jnp.bfloat16), keys, preferred_element_type=jnp.float32)
-            for k in range(PER_DOT):
-                rows = slice(k * BLOCK, k * BLOCK + BLOCK)
-                finish(first + k, weighted[rows], total[rows])
+            if first + PER_DOT < SOURCES:
+                score(first + PER_DOT)
+            rest(first)
 
 
 def finish_kernel(got_ref, wo_ref, feat_ref, position_ref, out_ref):
@@ -188,7 +199,7 @@
         pack_kernel,
         out_shape=shaped((HEADS, ROWS, 128), bf16),
         in_specs=[HBM] * 9,
-        out_specs=HBM,
+        out_specs=VMEM,
         scratch_shapes=[
             pltpu.VMEM((local_rows, width), bf16),
             pltpu.VMEM((1, width), f32),
@@ -200,15 +211,18 @@
             pltpu.VMEM((1, local_rows), i32),
             pltpu.VMEM((1, HEADS), f32),
             pltpu.VMEM((1, 128), i32),
-            pltpu.VMEM((HEADS, ROWS, 128), bf16),
             pltpu.SemaphoreType.DMA((9,)),
-            pltpu.SemaphoreType.DMA((HEADS,)),
         ],
         name="pack",
-        compiler_params=pltpu.CompilerParams(vmem_limit_bytes=60 << 20),
+        compiler_params=pltpu.CompilerParams(vmem_limit_bytes=12 << 20),
     )(
-        grid_feat, query_gain.reshape(1, -1), latent.T, w_kv, w_q, block_lists, list_len.reshape(1, 1),
-        dest.reshape(1, -1), head_scale.reshape(1, -1),
+        *(
+            pltpu.with_memory_space_constraint(x, pltpu.HBM)
+            for x in (grid_feat, query_gain.reshape(1, -1), latent.T, w_kv, w_q, block_lists)
+        ),
+        list_len.reshape(1, 1),
+        pltpu.with_memory_space_constraint(dest.reshape(1, -1), pltpu.HBM),
+        pltpu.with_memory_space_constraint(head_scale.reshape(1, -1), pltpu.HBM),
     )
     got = lax.all_to_all(packed, "y", 0, 0, tiled=True)
 
@@ -244,6 +258,8 @@
             pltpu.VMEM((SOURCES * BLOCK, LISTED * BLOCK), f32),
             pltpu.VMEM((SOURCES * BLOCK, LISTED * BLOCK), bf16),
             pltpu.VMEM((SOURCES * BLOCK, 128), f32),
+            pltpu.VMEM((HALF, GROUP * BLOCK), bf16),
+            pltpu.VMEM((GROUP * BLOCK, SOURCES * BLOCK), f32),
         ],
         name="attend",
         compiler_params=PARAMS,

time: 96.9 us -> 95.7 us (0.988)
  no operation moved by 1% of the time
where the time goes in v4:
time: 95.7 us; the launch traced here: 95.4 us
  blocking collectives  89.9 us (94%)
  Pallas kernels  4.11 us (4%)
    all_to_all x1, blocking collectives, shards(): panels = lax.all_to_all(panel, 'z', 0, 0, tiled=True)  25.7 us
    all_to_all x1, blocking collectives, shards(): arrived = lax.all_to_all(outgoing, ('xh', 'z', 'c'), 0, 0, tiled=True)  21.7 us
    all_to_all x1, blocking collectives, shards(): got = lax.all_to_all(packed, 'y', 0, 0, tiled=True)  18.8 us
    all_to_all x1, blocking collectives, shards(): attended = lax.all_to_all(attended, 'y', 0, 0, tiled=True)  10.5 us
    all_gather x1, blocking collectives, shards(): panels = lax.all_gather(panels, 'c', axis=0).reshape(GROUP, BLOCK, 128)  6.58 us
    all_gather x1, blocking collectives, shards(): parts = lax.all_gather(partial, 'xl', axis=0)  6.57 us

profile of v4, /device:TPU:1, one launch (start us, length us, event | category | flops | bytes accessed | tf_op | source)
XLA Modules:
  0.0 95.4 jit_solution(8133621696328632744)
XLA Ops:
  0.7 1.6 %pack.1 = bf16[8,200,128]{2,1,0:T(8,128)(2,1)S(1)} custom-call(bf16[128,512]{1,0:T(8,128)(2,1)} %feat_ref.1, f32[1,512]{1,0:T(1,128)} %bitcast.9, bf16[64,128]{1,0:T(8,128)(2,1)} %bitcast.8, bf16[64,1024]{1,0:T(8,128)(2,1)} %wkv_hbm.1, bf16[512,512]{1,0:T(8,128)(2,1)} %wq_hbm.1, s32[1,16]{1,0:T(1,128)} %list_hbm.1, s32[1,1]{1,0:T(1,128)} %bitcast.6.len_hbm, ...), custom_call_target="tpu_custom_call" | custom-call | tf_op jit(solution)/shard_map/pack/pallas_call | solution.py:198
  2.3 18.8 %all_to_all.20.got_ref = bf16[8,200,128]{2,1,0:T(8,128)(2,1)S(1)} all-to-all(bf16[8,200,128]{2,1,0:T(8,128)(2,1)S(1)} %pack.1), channel_id=1, replica_groups=mesh['xh'=4,'z'=8,'c'=2,'xl'=2,'y'=8] {'y'}, dimensions={0} | all-to-all | bytes 819200 | tf_op jit(solution)/shard_map/all_to_all | solution.py:227
  21.1 0.2 project.1
  21.3 6.6 %all-gather = f32[256,128]{1,0:T(8,128)S(1)} all-gather(f32[128,128]{1,0:T(8,128)S(1)} %get-tuple-element.11), channel_id=2, replica_groups=mesh['xh'=4,'z'=8,'c'=2,'xl'=2,'y'=8] {'xl'}, dimensions={0}, use_global_device_ids=true | all-gather | bytes 196608 | tf_op jit(solution)/shard_map/all_gather | solution.py:239
  27.9 25.7 %all_to_all.21 = bf16[8,128,128]{2,1,0:T(8,128)(2,1)S(1)} all-to-all(bf16[8,128,128]{2,1,0:T(8,128)(2,1)S(1)} %join.1), channel_id=1, replica_groups=mesh['xh'=4,'z'=8,'c'=2,'xl'=2,'y'=8] {'z'}, dimensions={0} | all-to-all | bytes 524288 | tf_op jit(solution)/shard_map/all_to_all | solution.py:248
  53.6 6.6 %all-gather.1.panel_ref = bf16[16,128,128]{2,1,0:T(8,128)(2,1)S(1)} all-gather(bf16[8,128,128]{2,1,0:T(8,128)(2,1)S(1)} %all_to_all.21), channel_id=3, replica_groups=mesh['xh'=4,'z'=8,'c'=2,'xl'=2,'y'=8] {'c'}, dimensions={0}, use_global_device_ids=true | all-gather | bytes 786432 | tf_op jit(solution)/shard_map/all_gather | solution.py:249
  60.2 0.0 copy-start.1
  60.2 1.7 %attend.1 = bf16[8,64,128]{2,1,0:T(8,128)(2,1)S(1)} custom-call(s32[8,128]{1,0:T(8,128)S(1)} %get-tuple-element.9.table_ref, f32[1,128]{1,0:T(1,128)S(1)} %get-tuple-element.10.scale_ref, bf16[8,200,128]{2,1,0:T(8,128)(2,1)S(1)} %all_to_all.20.got_ref, bf16[16,128,128]{2,1,0:T(8,128)(2,1)S(1)} %all-gather.1.panel_ref), custom_call_target="tpu_custom_call" | custom-call | tf_op jit(solution)/shard_map/attend/pallas_call | solution.py:251
  61.9 0.0 copy-start
  61.9 10.5 %all_to_all.22.got_ref = bf16[8,64,128]{2,1,0:T(8,128)(2,1)S(1)} all-to-all(bf16[8,64,128]{2,1,0:T(8,128)(2,1)S(1)} %attend.1), channel_id=1, replica_groups=mesh['xh'=4,'z'=8,'c'=2,'xl'=2,'y'=8] {'y'}, dimensions={0} | all-to-all | bytes 262144 | tf_op jit(solution)/shard_map/all_to_all | solution.py:267
  72.4 0.0 copy-done.1
  72.4 0.0 copy-done
  72.4 0.5 finish.1
  73.0 21.7 %all_to_all.23 = bf16[64,2,512]{2,1,0:T(2,128)(2,1)S(1)} all-to-all(bf16[64,2,512]{2,1,0:T(2,128)(2,1)S(1)} %finish.1), channel_id=1, replica_groups=mesh['xh'=4,'z'=8,'c'=2,'xl'=2,'y'=8] {'xh','z','c'}, dimensions={0} | all-to-all | bytes 262144 | tf_op jit(solution)/shard_map/all_to_all | solution.py:277
  94.7 0.7 reshape.23
  (1 shorter events, 0.0 us)
Async XLA Ops:
  60.2 12.3 %copy-start.1 = (bf16[512,512]{1,0:T(8,128)(2,1)S(1)}, bf16[512,512]{1,0:T(8,128)(2,1)}, u32[]{:S(2)}) copy-start(bf16[512,512]{1,0:T(8,128)(2,1)} %wo_ref.1) | copy-start | bytes 1572868
  61.9 10.6 %copy-start = (bf16[128,512]{1,0:T(8,128)(2,1)S(1)}, bf16[128,512]{1,0:T(8,128)(2,1)}, u32[]{:S(2)}) copy-start(bf16[128,512]{1,0:T(8,128)(2,1)} %feat_ref.1) | copy-start | bytes 393220

commit v5 on v4

--- a/solution.py
+++ b/solution.py
@@ -20,7 +20,7 @@
 PER_DOT = 4
 
 VMEM = pl.BlockSpec(memory_space=pltpu.VMEM)
-SMEM = pl.BlockSpec(memory_space=pltpu.SMEM)
+ANY = pl.BlockSpec(memory_space=pl.ANY)
 HBM = pl.BlockSpec(memory_space=pltpu.HBM)
 PARAMS = pltpu.CompilerParams(vmem_limit_bytes=24 << 20)
 CONTRACT_LAST = (((1,), (1,)), ((), ()))
@@ -52,6 +52,17 @@
     centred = values - jnp.mean(values, axis=-1, keepdims=True)
     spread = jnp.mean(centred * centred, axis=-1, keepdims=True)
     normed = (centred * lax.rsqrt(spread + 1e-05) * gain_ref[...]).astype(jnp.bfloat16)
+    low = low_lanes(HALF)
+    for head in range(HEADS):
+        tile = slice(head // 2 * 128, head // 2 * 128 + 128)
+        keys = wkv_ref[:, tile]
+        values = wkv_ref[:, slice(tile.start + 512, tile.stop + 512)]
+        if head % 2:
+            keys = swap_halves(keys)
+        else:
+            values = swap_halves(values)
+        out_ref[head, 0:HALF] = lat_ref[...]
+        out_ref[head, HALF:2 * HALF] = jnp.where(low, keys, values)
     for copy in copies[4:]:
         copy.wait()
     queries = jnp.dot(normed, wq_ref[...], preferred_element_type=jnp.float32).astype(jnp.bfloat16)
@@ -70,18 +81,13 @@
     second = (own - first).astype(jnp.bfloat16).astype(jnp.float32)
     parts = jnp.where(row == 2, first, jnp.where(row == 3, second, own - first - second))
     entries = jnp.where(row < 2, entries.astype(jnp.float32), parts).astype(jnp.bfloat16)
-    low = low_lanes(HALF)
     for head in range(HEADS):
         tile = slice(head // 2 * 128, head // 2 * 128 + 128)
-        keys = wkv_ref[:, tile]
-        values = wkv_ref[:, slice(tile.start + 512, tile.stop + 512)]
         upper, lower = queries[0:HALF, tile], queries[HALF:BLOCK, tile]
         if head % 2:
-            keys, upper = swap_halves(keys), swap_halves(upper)
+            upper = swap_halves(upper)
         else:
-            values, lower = swap_halves(values), swap_halves(lower)
-        out_ref[head, 0:HALF] = lat_ref[...]
-        out_ref[head, HALF:2 * HALF] = jnp.where(low, keys, values)
+            lower = swap_halves(lower)
         out_ref[head, 2 * HALF:TAIL] = jnp.where(low, upper, lower)
         out_ref[head, TAIL:ROWS] = entries
 
@@ -106,7 +112,12 @@
         out_ref[peer] = panel
 
 
-def attend_kernel(table_ref, scale_ref, got_ref, panel_ref, out_ref, query_ref, score_ref, prob_ref, total_ref, values_ref, full_ref):
+def attend_kernel(
+    table_any, scale_ref, got_ref, panel_ref, out_ref,
+    query_ref, score_ref, prob_ref, total_ref, values_ref, full_ref, table_ref, sem,
+):
+    fetch = pltpu.make_async_copy(table_any, table_ref, sem)
+    fetch.start()
     scale = scale_ref[:, 0:1] * (math.log2(math.e) / math.sqrt(HEAD_DIM))
     low = low_lanes(HALF)
     for source in range(SOURCES):
@@ -122,6 +133,7 @@
     def blocks_of(source):
         return jnp.concatenate([panel_ref[table_ref[source, j]] for j in range(LISTED)], axis=0)
 
+    fetch.wait()
     dense = table_ref[0, GROUP] > LISTED * BLOCK
 
     @pl.when(jnp.logical_not(dense))
@@ -251,7 +263,7 @@
     attended = pl.pallas_call(
         attend_kernel,
         out_shape=shaped((SOURCES, HALF, 128), bf16),
-        in_specs=[SMEM, VMEM, VMEM, VMEM],
+        in_specs=[ANY, VMEM, VMEM, VMEM],
         out_specs=VMEM,
         scratch_shapes=[
             pltpu.VMEM((SOURCES * BLOCK, 128), bf16),
@@ -260,6 +272,8 @@
             pltpu.VMEM((SOURCES * BLOCK, 128), f32),
             pltpu.VMEM((HALF, GROUP * BLOCK), bf16),
             pltpu.VMEM((GROUP * BLOCK, SOURCES * BLOCK), f32),
+            pltpu.SMEM((SOURCES, 128), i32),
+            pltpu.SemaphoreType.DMA,
         ],
         name="attend",
         compiler_params=PARAMS,

time: 95.7 us -> 95.6 us (level)
  no operation moved by 1% of the time
where the time goes in v5:
time: 95.6 us; the launch traced here: 95.3 us
  blocking collectives  89.9 us (94%)
  Pallas kernels  4.04 us (4%)
    all_to_all x1, blocking collectives, shards(): panels = lax.all_to_all(panel, 'z', 0, 0, tiled=True)  25.7 us
    all_to_all x1, blocking collectives, shards(): arrived = lax.all_to_all(outgoing, ('xh', 'z', 'c'), 0, 0, tiled=True)  21.7 us
    all_to_all x1, blocking collectives, shards(): got = lax.all_to_all(packed, 'y', 0, 0, tiled=True)  18.8 us
    all_to_all x1, blocking collectives, shards(): attended = lax.all_to_all(attended, 'y', 0, 0, tiled=True)  10.5 us
    all_gather x1, blocking collectives, shards(): panels = lax.all_gather(panels, 'c', axis=0).reshape(GROUP, BLOCK, 128)  6.58 us
    all_gather x1, blocking collectives, shards(): parts = lax.all_gather(partial, 'xl', axis=0)  6.58 us

profile of v5, /device:TPU:1, one launch (start us, length us, event | category | flops | bytes accessed | tf_op | source)
XLA Modules:
  0.0 95.3 jit_solution(15275870461637284398)
XLA Ops:
  0.7 1.6 %pack.1 = bf16[8,200,128]{2,1,0:T(8,128)(2,1)S(1)} custom-call(bf16[128,512]{1,0:T(8,128)(2,1)} %feat_ref.1, f32[1,512]{1,0:T(1,128)} %bitcast.9, bf16[64,128]{1,0:T(8,128)(2,1)} %bitcast.8, bf16[64,1024]{1,0:T(8,128)(2,1)} %wkv_hbm.1, bf16[512,512]{1,0:T(8,128)(2,1)} %wq_hbm.1, s32[1,16]{1,0:T(1,128)} %list_hbm.1, s32[1,1]{1,0:T(1,128)} %bitcast.6.len_hbm, ...), custom_call_target="tpu_custom_call" | custom-call | tf_op jit(solution)/shard_map/pack/pallas_call | solution.py:210
  2.3 18.8 %all_to_all.20.got_ref = bf16[8,200,128]{2,1,0:T(8,128)(2,1)S(1)} all-to-all(bf16[8,200,128]{2,1,0:T(8,128)(2,1)S(1)} %pack.1), channel_id=1, replica_groups=mesh['xh'=4,'z'=8,'c'=2,'xl'=2,'y'=8] {'y'}, dimensions={0} | all-to-all | bytes 819200 | tf_op jit(solution)/shard_map/all_to_all | solution.py:239
  21.1 0.2 project.1
  21.3 6.6 %all-gather = f32[256,128]{1,0:T(8,128)S(1)} all-gather(f32[128,128]{1,0:T(8,128)S(1)} %get-tuple-element.11), channel_id=2, replica_groups=mesh['xh'=4,'z'=8,'c'=2,'xl'=2,'y'=8] {'xl'}, dimensions={0}, use_global_device_ids=true | all-gather | bytes 196608 | tf_op jit(solution)/shard_map/all_gather | solution.py:251
  27.9 25.7 %all_to_all.21 = bf16[8,128,128]{2,1,0:T(8,128)(2,1)S(1)} all-to-all(bf16[8,128,128]{2,1,0:T(8,128)(2,1)S(1)} %join.1), channel_id=1, replica_groups=mesh['xh'=4,'z'=8,'c'=2,'xl'=2,'y'=8] {'z'}, dimensions={0} | all-to-all | bytes 524288 | tf_op jit(solution)/shard_map/all_to_all | solution.py:260
  53.6 6.6 %all-gather.1.panel_ref = bf16[16,128,128]{2,1,0:T(8,128)(2,1)S(1)} all-gather(bf16[8,128,128]{2,1,0:T(8,128)(2,1)S(1)} %all_to_all.21), channel_id=3, replica_groups=mesh['xh'=4,'z'=8,'c'=2,'xl'=2,'y'=8] {'c'}, dimensions={0}, use_global_device_ids=true | all-gather | bytes 786432 | tf_op jit(solution)/shard_map/all_gather | solution.py:261
  60.2 0.0 copy-start.1
  60.2 1.7 %attend.1 = bf16[8,64,128]{2,1,0:T(8,128)(2,1)S(1)} custom-call(s32[8,128]{1,0:T(8,128)S(1)} %get-tuple-element.9.table_any, f32[1,128]{1,0:T(1,128)S(1)} %get-tuple-element.10.scale_ref, bf16[8,200,128]{2,1,0:T(8,128)(2,1)S(1)} %all_to_all.20.got_ref, bf16[16,128,128]{2,1,0:T(8,128)(2,1)S(1)} %all-gather.1.panel_ref), custom_call_target="tpu_custom_call" | custom-call | tf_op jit(solution)/shard_map/attend/pallas_call | solution.py:263
  61.8 0.0 copy-start
  61.8 10.5 %all_to_all.22.got_ref = bf16[8,64,128]{2,1,0:T(8,128)(2,1)S(1)} all-to-all(bf16[8,64,128]{2,1,0:T(8,128)(2,1)S(1)} %attend.1), channel_id=1, replica_groups=mesh['xh'=4,'z'=8,'c'=2,'xl'=2,'y'=8] {'y'}, dimensions={0} | all-to-all | bytes 262144 | tf_op jit(solution)/shard_map/all_to_all | solution.py:281
  72.4 0.0 copy-done.1
  72.4 0.0 copy-done
  72.4 0.5 finish.1
  72.9 21.7 %all_to_all.23 = bf16[64,2,512]{2,1,0:T(2,128)(2,1)S(1)} all-to-all(bf16[64,2,512]{2,1,0:T(2,128)(2,1)S(1)} %finish.1), channel_id=1, replica_groups=mesh['xh'=4,'z'=8,'c'=2,'xl'=2,'y'=8] {'xh','z','c'}, dimensions={0} | all-to-all | bytes 262144 | tf_op jit(solution)/shard_map/all_to_all | solution.py:291
  94.6 0.7 reshape.23
  (1 shorter events, 0.0 us)
Async XLA Ops:
  60.2 12.2 %copy-start.1 = (bf16[512,512]{1,0:T(8,128)(2,1)S(1)}, bf16[512,512]{1,0:T(8,128)(2,1)}, u32[]{:S(2)}) copy-start(bf16[512,512]{1,0:T(8,128)(2,1)} %wo_ref.1) | copy-start | bytes 1572868
  61.8 10.6 %copy-start = (bf16[128,512]{1,0:T(8,128)(2,1)S(1)}, bf16[128,512]{1,0:T(8,128)(2,1)}, u32[]{:S(2)}) copy-start(bf16[128,512]{1,0:T(8,128)(2,1)} %feat_ref.1) | copy-start | bytes 393220

commit v6 on v5

--- a/solution.py
+++ b/solution.py
@@ -18,6 +18,7 @@
 ROWS = 200
 TAIL = 3 * HALF
 PER_DOT = 4
+CHUNK = 16
 
 VMEM = pl.BlockSpec(memory_space=pltpu.VMEM)
 ANY = pl.BlockSpec(memory_space=pl.ANY)
@@ -133,6 +134,9 @@
     def blocks_of(source):
         return jnp.concatenate([panel_ref[table_ref[source, j]] for j in range(LISTED)], axis=0)
 
+    for block in range(GROUP):
+        turned = jnp.transpose(panel_ref[block].astype(jnp.float32))
+        values_ref[block] = turned[HALF:BLOCK].astype(jnp.bfloat16)
     fetch.wait()
     dense = table_ref[0, GROUP] > LISTED * BLOCK
 
@@ -156,34 +160,38 @@
 
     @pl.when(dense)
     def _():
-        keys = panel_ref[...].reshape(GROUP * BLOCK, 128)
         span = PER_DOT * BLOCK
-
-        def score(first):
+        chunks = range(0, GROUP, CHUNK)
+
+        def score(first, chunk):
             query = query_ref[first * BLOCK:first * BLOCK + span]
-            full_ref[:, first * BLOCK:first * BLOCK + span] = lax.dot_general(
+            keys = panel_ref[chunk:chunk + CHUNK].reshape(CHUNK * BLOCK, 128)
+            rows = slice(chunk * BLOCK, (chunk + CHUNK) * BLOCK)
+            full_ref[rows, first * BLOCK:first * BLOCK + span] = lax.dot_general(
                 keys, query, CONTRACT_LAST, preferred_element_type=jnp.float32
             )
 
-        def rest(first):
-            scores = full_ref[:, first * BLOCK:first * BLOCK + span]
-            weights = jnp.exp2((scores - jnp.max(scores, axis=0, keepdims=True)) * scale)
-            total = jnp.sum(weights, axis=0, keepdims=True)
-            weighted = jnp.dot(values_ref[...], weights.astype(jnp.bfloat16), preferred_element_type=jnp.float32)
+        for chunk in chunks:
+            score(0, chunk)
+        for first in range(0, SOURCES, PER_DOT):
+            columns = slice(first * BLOCK, first * BLOCK + span)
+            top = jnp.max(full_ref[:, columns], axis=0, keepdims=True)
+            total, weighted = 0.0, 0.0
+            for chunk in chunks:
+                rows = slice(chunk * BLOCK, (chunk + CHUNK) * BLOCK)
+                if first + PER_DOT < SOURCES:
+                    score(first + PER_DOT, chunk)
+                weights = jnp.exp2((full_ref[rows, columns] - top) * scale)
+                total = total + jnp.sum(weights, axis=0, keepdims=True)
+                values = jnp.concatenate([values_ref[chunk + k] for k in range(CHUNK)], axis=1)
+                weighted = weighted + jnp.dot(
+                    values, weights.astype(jnp.bfloat16), preferred_element_type=jnp.float32
+                )
             attended = weighted / total
             for k in range(PER_DOT):
                 piece = attended[:, k * BLOCK:k * BLOCK + BLOCK]
                 piece = jnp.transpose(jnp.concatenate([piece, swap_halves(piece)], axis=0))
                 out_ref[first + k] = piece[0:HALF].astype(jnp.bfloat16)
-
-        score(0)
-        for block in range(GROUP):
-            turned = jnp.transpose(panel_ref[block].astype(jnp.float32))
-            values_ref[:, block * BLOCK:block * BLOCK + BLOCK] = turned[HALF:BLOCK].astype(jnp.bfloat16)
-        for first in range(0, SOURCES, PER_DOT):
-            if first + PER_DOT < SOURCES:
-                score(first + PER_DOT)
-            rest(first)
 
 
 def finish_kernel(got_ref, wo_ref, feat_ref, position_ref, out_ref):
@@ -270,7 +278,7 @@
             pltpu.VMEM((SOURCES * BLOCK, LISTED * BLOCK), f32),
             pltpu.VMEM((SOURCES * BLOCK, LISTED * BLOCK), bf16),
             pltpu.VMEM((SOURCES * BLOCK, 128), f32),
-            pltpu.VMEM((HALF, GROUP * BLOCK), bf16),
+            pltpu.VMEM((GROUP, HALF, BLOCK), bf16),
             pltpu.VMEM((GROUP * BLOCK, SOURCES * BLOCK), f32),
             pltpu.SMEM((SOURCES, 128), i32),
             pltpu.SemaphoreType.DMA,

time: 95.6 us -> 95.6 us (level)
  no operation moved by 1% of the time
where the time goes in v6:
time: 95.6 us; the launch traced here: 95.3 us
  blocking collectives  89.9 us (94%)
  Pallas kernels  4.03 us (4%)
    all_to_all x1, blocking collectives, shards(): panels = lax.all_to_all(panel, 'z', 0, 0, tiled=True)  25.7 us
    all_to_all x1, blocking collectives, shards(): arrived = lax.all_to_all(outgoing, ('xh', 'z', 'c'), 0, 0, tiled=True)  21.7 us
    all_to_all x1, blocking collectives, shards(): got = lax.all_to_all(packed, 'y', 0, 0, tiled=True)  18.8 us
    all_to_all x1, blocking collectives, shards(): attended = lax.all_to_all(attended, 'y', 0, 0, tiled=True)  10.5 us
    all_gather x1, blocking collectives, shards(): panels = lax.all_gather(panels, 'c', axis=0).reshape(GROUP, BLOCK, 128)  6.58 us
    all_gather x1, blocking collectives, shards(): parts = lax.all_gather(partial, 'xl', axis=0)  6.58 us

profile of v6, /device:TPU:1, one launch (start us, length us, event | category | flops | bytes accessed | tf_op | source)
XLA Modules:
  0.0 95.3 jit_solution(7784689570059371478)
XLA Ops:
  0.7 1.6 %pack.1 = bf16[8,200,128]{2,1,0:T(8,128)(2,1)S(1)} custom-call(bf16[128,512]{1,0:T(8,128)(2,1)} %feat_ref.1, f32[1,512]{1,0:T(1,128)} %bitcast.9, bf16[64,128]{1,0:T(8,128)(2,1)} %bitcast.8, bf16[64,1024]{1,0:T(8,128)(2,1)} %wkv_hbm.1, bf16[512,512]{1,0:T(8,128)(2,1)} %wq_hbm.1, s32[1,16]{1,0:T(1,128)} %list_hbm.1, s32[1,1]{1,0:T(1,128)} %bitcast.6.len_hbm, ...), custom_call_target="tpu_custom_call" | custom-call | tf_op jit(solution)/shard_map/pack/pallas_call | solution.py:218
  2.3 18.8 %all_to_all.20.got_ref = bf16[8,200,128]{2,1,0:T(8,128)(2,1)S(1)} all-to-all(bf16[8,200,128]{2,1,0:T(8,128)(2,1)S(1)} %pack.1), channel_id=1, replica_groups=mesh['xh'=4,'z'=8,'c'=2,'xl'=2,'y'=8] {'y'}, dimensions={0} | all-to-all | bytes 819200 | tf_op jit(solution)/shard_map/all_to_all | solution.py:247
  21.1 0.2 project.1
  21.3 6.6 %all-gather = f32[256,128]{1,0:T(8,128)S(1)} all-gather(f32[128,128]{1,0:T(8,128)S(1)} %get-tuple-element.11), channel_id=2, replica_groups=mesh['xh'=4,'z'=8,'c'=2,'xl'=2,'y'=8] {'xl'}, dimensions={0}, use_global_device_ids=true | all-gather | bytes 196608 | tf_op jit(solution)/shard_map/all_gather | solution.py:259
  27.9 25.7 %all_to_all.21 = bf16[8,128,128]{2,1,0:T(8,128)(2,1)S(1)} all-to-all(bf16[8,128,128]{2,1,0:T(8,128)(2,1)S(1)} %join.1), channel_id=1, replica_groups=mesh['xh'=4,'z'=8,'c'=2,'xl'=2,'y'=8] {'z'}, dimensions={0} | all-to-all | bytes 524288 | tf_op jit(solution)/shard_map/all_to_all | solution.py:268
  53.6 6.6 %all-gather.1.panel_ref = bf16[16,128,128]{2,1,0:T(8,128)(2,1)S(1)} all-gather(bf16[8,128,128]{2,1,0:T(8,128)(2,1)S(1)} %all_to_all.21), channel_id=3, replica_groups=mesh['xh'=4,'z'=8,'c'=2,'xl'=2,'y'=8] {'c'}, dimensions={0}, use_global_device_ids=true | all-gather | bytes 786432 | tf_op jit(solution)/shard_map/all_gather | solution.py:269
  60.2 0.0 copy-start.1
  60.2 1.7 %attend.1 = bf16[8,64,128]{2,1,0:T(8,128)(2,1)S(1)} custom-call(s32[8,128]{1,0:T(8,128)S(1)} %get-tuple-element.9.table_any, f32[1,128]{1,0:T(1,128)S(1)} %get-tuple-element.10.scale_ref, bf16[8,200,128]{2,1,0:T(8,128)(2,1)S(1)} %all_to_all.20.got_ref, bf16[16,128,128]{2,1,0:T(8,128)(2,1)S(1)} %all-gather.1.panel_ref), custom_call_target="tpu_custom_call" | custom-call | tf_op jit(solution)/shard_map/attend/pallas_call | solution.py:271
  61.8 0.0 copy-start
  61.8 10.5 %all_to_all.22.got_ref = bf16[8,64,128]{2,1,0:T(8,128)(2,1)S(1)} all-to-all(bf16[8,64,128]{2,1,0:T(8,128)(2,1)S(1)} %attend.1), channel_id=1, replica_groups=mesh['xh'=4,'z'=8,'c'=2,'xl'=2,'y'=8] {'y'}, dimensions={0} | all-to-all | bytes 262144 | tf_op jit(solution)/shard_map/all_to_all | solution.py:289
  72.4 0.0 copy-done.1
  72.4 0.0 copy-done
  72.4 0.5 finish.1
  72.9 21.7 %all_to_all.23 = bf16[64,2,512]{2,1,0:T(2,128)(2,1)S(1)} all-to-all(bf16[64,2,512]{2,1,0:T(2,128)(2,1)S(1)} %finish.1), channel_id=1, replica_groups=mesh['xh'=4,'z'=8,'c'=2,'xl'=2,'y'=8] {'xh','z','c'}, dimensions={0} | all-to-all | bytes 262144 | tf_op jit(solution)/shard_map/all_to_all | solution.py:299
  94.6 0.7 reshape.23
  (1 shorter events, 0.0 us)
Async XLA Ops:
  60.2 12.2 %copy-start.1 = (bf16[512,512]{1,0:T(8,128)(2,1)S(1)}, bf16[512,512]{1,0:T(8,128)(2,1)}, u32[]{:S(2)}) copy-start(bf16[512,512]{1,0:T(8,128)(2,1)} %wo_ref.1) | copy-start | bytes 1572868
  61.8 10.6 %copy-start = (bf16[128,512]{1,0:T(8,128)(2,1)S(1)}, bf16[128,512]{1,0:T(8,128)(2,1)}, u32[]{:S(2)}) copy-start(bf16[128,512]{1,0:T(8,128)(2,1)} %feat_ref.1) | copy-start | bytes 393220
